TPU v7x, 128 devices: a whole 4x4x4 slice. The times are simulated.
128 devices in a mesh: sub: 8 (over z_hi, x), beam: 16 (over z_lo, y, core).
Axes of the slice: x: 4, y: 4, z: 4 (z_hi: 2, z_lo: 2; z = z_hi * 2 + z_lo), core: 2. Of those that a mesh axis runs over, the one named last changes fastest.
Arguments:
- voltages: bfloat16 [1024, 256, 2, 1024], P(('sub', 'beam')), may hold values from -6 to 6
- weights: bfloat16 [256, 2, 1024, 1024], P(('sub', 'beam')), may hold values from -0.1875 to 0.1875
- antenna_map: int32 [1024], replicated, may hold values from 0 to 1023, each once
- delays: int32 [256, 32], P('sub'), may hold values from 0 to 127, as said below
Outputs:
- filterbank: bfloat16 [256, 1024, 256], P('sub', 'beam')
- series: float32 [32, 1024, 128], P('sub', 'beam')
Inputs may be any that keep to these rules, and one draw needn't show every extreme that they name: antenna_map is a permutation of the antennas. delays never rise with the channel and never fall with the trial; trial 0 has no delay.
All inputs are finite; a program needn't handle non-finite values.
Results may differ from a plain program's by a relative error of at most 0.008.
Values may be sent and summed in bfloat16 or wider, within the bound.
No kernel may reach another device: no remote copies, remote signals or barrier semaphores. Data moves between devices by JAX's collectives and lax.ppermute only.
A program may use at most 64 MiB of HBM per device.

v0:
```python
import math

import jax
import jax.numpy as jnp
from jax import lax
from jax.sharding import PartitionSpec as P

A = 1024
NFFT = 1024
C = 256
TRIALS = 32
OUT = 128


def cut_along(x, dim, devices):
    before, after = (x.shape[:dim], x.shape[dim + 1 :])
    return jnp.moveaxis(x.reshape(*before, devices, -1, *after), dim, 0)


def sum_at_owner(x, axis, dim):
    devices = lax.axis_size(axis)
    pieces = lax.all_to_all(cut_along(x, dim, devices), axis, 0, 0, tiled=True)
    return jnp.sum(pieces.astype(jnp.float32), axis=0)


def dft_table():
    sample = jnp.arange(NFFT, dtype=jnp.int32)
    channel = jnp.arange(C, dtype=jnp.int32)
    turns = channel[:, None] * sample[None, :] % NFFT
    phase = turns.astype(jnp.float32) * (2.0 * math.pi / NFFT)
    cosine = jnp.cos(phase) / math.sqrt(NFFT)
    sine = jnp.sin(phase) / math.sqrt(NFFT)
    real_row = jnp.stack([cosine, sine], axis=1)
    imag_row = jnp.stack([-sine, cosine], axis=1)
    return jnp.stack([real_row, imag_row], axis=0).astype(jnp.bfloat16)


def on_device(voltages, weights, antenna_map, delays):
    antenna_per_device = voltages.shape[0]
    frame_count = voltages.shape[1]
    local_spectra = jnp.einsum(
        "ocin,afin->aocf", dft_table(), voltages, preferred_element_type=jnp.float32
    ).astype(jnp.bfloat16)
    subband_count = lax.axis_size("sub")
    beam_count = lax.axis_size("beam")
    owned_channels = C // (subband_count * beam_count)
    direct_path = local_spectra.reshape(
        1, antenna_per_device, 2, subband_count * beam_count, owned_channels, frame_count
    )
    moved = lax.all_to_all(direct_path, ("sub", "beam"), split_axis=3, concat_axis=0, tiled=True)
    spectra = moved.reshape(A, 2, owned_channels, frame_count)
    inverse = jnp.zeros((A,), jnp.int32).at[antenna_map].set(jnp.arange(A, dtype=jnp.int32))
    by_antenna = jnp.take(spectra, inverse, axis=0)
    products = jnp.einsum(
        "cjba,aicf->cjibf", weights, by_antenna, preferred_element_type=jnp.float32
    )
    beam_re = products[:, 0, 0] - products[:, 1, 1]
    beam_im = products[:, 0, 1] + products[:, 1, 0]
    power = (beam_re * beam_re + beam_im * beam_im).astype(jnp.bfloat16)
    filterbank = lax.all_to_all(power, "beam", split_axis=1, concat_axis=0, tiled=True)
    sub_channels = filterbank.shape[0]
    beams_here = filterbank.shape[1]
    channel_block = 4
    frame_pos = jnp.arange(frame_count, dtype=jnp.int32)
    out_pos = jnp.arange(OUT, dtype=jnp.int32)

    def add_block(block_index, total):
        start = block_index * channel_block
        spectra_piece = lax.dynamic_slice_in_dim(filterbank, start, channel_block, 0)
        shifts = lax.dynamic_slice_in_dim(delays, start, channel_block, 0)
        channel_selector = (
            frame_pos[None, :, None, None]
            == out_pos[None, None, None, :] + shifts[:, None, :, None]
        ).astype(jnp.bfloat16)
        return total + jnp.einsum(
            "jsv,jvra->rsa", spectra_piece, channel_selector, preferred_element_type=jnp.float32
        )

    start_total = jnp.zeros((TRIALS, beams_here, OUT), jnp.float32)
    total = lax.fori_loop(0, sub_channels // channel_block, add_block, start_total)
    series = sum_at_owner((total * (1.0 / C)).astype(jnp.bfloat16), "sub", 0)
    return (filterbank, series)


def solution(mesh):
    placed = (
        P(("sub", "beam"), None, None, None),
        P(("sub", "beam"), None, None, None),
        P(),
        P("sub", None),
    )
    return jax.shard_map(
        on_device,
        mesh=mesh,
        in_specs=placed,
        out_specs=(P("sub", "beam", None), P("sub", "beam", None)),
        check_vma=False,
    )
```

profile of v0, /device:TPU:0, one launch (start us, length us, event | category | flops | bytes accessed | tf_op | source)
XLA Modules:
  0.0 161.6 jit_solution(8345779969694855784)
XLA Ops:
  0.6 4.3 %negate_convert_fusion = (bf16[256,1,1024]{2,0,1:T(8,128)(2,1)S(1)}, bf16[256,1,1024]{2,0,1:T(8,128)(2,1)S(1)}) fusion(), kind=kLoop, calls=%fused_computation.45 | loop fusion | flops 4980736 | bytes 1048576 | tf_op jit(solution)/shard_map/convert.3
  5.0 4.0 %fusion.39 = bf16[256,1,1024]{2,0,1:T(8,128)(2,1)S(1)} fusion(), kind=kLoop, calls=%fused_computation.52 | loop fusion | flops 4194304 | bytes 524288 | tf_op jit(solution)/shard_map/convert.7
  8.9 0.2 maximum_bitcast_fusion.4
  9.1 10.2 %fusion.29 = bf16[8,2,256,256]{3,2,0,1:T(8,128)(2,1)} fusion(bf16[8,256,2,1024]{3,2,1,0:T(2,128)(2,1)} %param.6, bf16[1,256,2,1024]{3,1,2,0:T(8,128)(2,1)S(1)} %get-tuple-element.156, bf16[1,256,2,1024]{3,1,2,0:T(8,128)(2,1)S(1)} %get-tuple-element.155), kind=kOutput, calls=%fused_computation.34 | convolution fusion | flops 4300210176 | bytes 12582912 | tf_op jit(solution)/shard_map/ocin,afin->aocf/dot_general | solution.py:41
  19.4 2.7 %reshape.115 = bf16[1,8,2,128,2,256]{5,4,3,1,2,0:T(2,128)(2,1)S(1)} reshape(bf16[8,2,256,256]{3,2,0,1:T(8,128)(2,1)} %fusion.29) | data formatting | bytes 4194304 | tf_op jit(solution)/shard_map/reshape | solution.py:47
  22.1 3.6 %copy.23 = bf16[1,8,2,128,2,256]{5,1,4,2,0,3:T(8,128)(2,1)} copy(bf16[1,8,2,128,2,256]{5,4,3,1,2,0:T(2,128)(2,1)S(1)} %reshape.115) | data formatting | bytes 4194304 | tf_op jit(solution)/shard_map/reshape | solution.py:47
  25.7 0.0 copy-start.1
  25.7 11.2 %all-to-all-start = ((bf16[1,8,2,128,2,256]{5,1,4,2,0,3:T(8,128)(2,1)}), bf16[1,8,2,128,2,256]{5,1,4,2,0,3:T(8,128)(2,1)S(1)}, u32[]{:S(2)}, u32[]{:S(2)}) async-start(bf16[1,8,2,128,2,256]{5,1,4,2,0,3:T(8,128)(2,1)} %copy.23), calls=%async_computation | async-start | bytes 4194304 | tf_op jit(solution)/shard_map/all_to_all | solution.py:50
  36.9 0.0 copy-done.1
  36.9 4.5 %scatter_custom_fusion = s32[1024]{0:T(1024)S(1)} fusion(s32[1024]{0:T(1024)S(1)} %compare_select_fusion.1, s32[1024]{0:T(1024)S(1)} %iota.33, s32[]{:T(128)} %constant.62.clone.1), kind=kCustom, calls=%fused_computation.57 | custom fusion | bytes 4100 | tf_op jit(solution)/shard_map/scatter | solution.py:52
  41.4 25.8 %all-to-all-done = bf16[1,8,2,128,2,256]{5,1,4,2,0,3:T(8,128)(2,1)S(1)} async-done(((bf16[1,8,2,128,2,256]{5,1,4,2,0,3:T(8,128)(2,1)}), bf16[1,8,2,128,2,256]{5,1,4,2,0,3:T(8,128)(2,1)S(1)}, u32[]{:S(2)}, u32[]{:S(2)}) %all-to-all-start) | async-done | bytes 2097184 | tf_op jit(solution)/shard_map/all_to_all | solution.py:50
  67.2 0.1 copy.50
  67.3 3.5 %copy.25 = bf16[1024,2,2,256]{3,2,1,0:T(2,128)(2,1)} copy(bf16[1024,2,2,256]{3,0,2,1:T(8,128)(2,1)S(1)} %bitcast.68) | data formatting | bytes 4194304 | tf_op jit(solution)/shard_map/reshape | solution.py:51
  70.8 7.9 %gather_fusion = bf16[1024,2,2,256]{3,2,1,0:T(2,128)(2,1)S(1)} fusion(bf16[1024,2,2,256]{3,2,1,0:T(2,128)(2,1)} %copy.25, s32[1024]{0:T(1024)S(1)} %fusion.40), kind=kCustom, calls=%fused_computation | custom fusion | bytes 4198400 | tf_op jit(solution)/shard_map/jit(_take)/gather | solution.py:53
  78.7 3.9 %fusion.28 = bf16[1024,2,2,256,1]{3,2,1,0,4:T(2,128)(2,1)S(1)} fusion(bf16[1024,2,2,256]{3,2,1,0:T(2,128)(2,1)S(1)} %gather_fusion, pred[1024]{0:T(1024)(128)(4,1)S(1)} %compare_and_fusion), kind=kLoop, calls=%fused_computation.33 | loop fusion | flops 1048576 | bytes 4195328 | tf_op jit(solution)/shard_map/jit(_take)/select_n | solution.py:53
  82.7 7.6 %fusion.16 = f32[2,2,2,1024,256]{3,4,1,2,0:T(8,128)S(1)} fusion(bf16[2,2,1024,1024]{3,2,1,0:T(8,128)(2,1)} %param.7, bf16[1024,2,2,256,1]{3,2,1,0,4:T(2,128)(2,1)S(1)} %fusion.28), kind=kOutput, calls=%fused_computation.21 | convolution fusion | flops 4294967296 | bytes 18874368 | tf_op jit(solution)/shard_map/cjba,aicf->cjibf/dot_general | solution.py:54
  90.2 1.0 fusion.37
  91.3 2.0 %copy.27 = bf16[2,1024,256]{2,0,1:T(2,128)(2,1)} copy(bf16[2,1024,256]{1,2,0:T(8,128)(2,1)S(1)} %fusion.37) | data formatting | bytes 2097152 | tf_op jit(solution)/shard_map/convert_element_type | solution.py:59
  93.3 3.7 %all-to-all-start.1 = ((bf16[2,1024,256]{2,0,1:T(2,128)(2,1)}), bf16[2,1024,256]{2,0,1:T(2,128)(2,1)S(1)}, u32[]{:S(2)}, u32[]{:S(2)}) async-start(bf16[2,1024,256]{2,0,1:T(2,128)(2,1)} %copy.27), calls=%async_computation.1 | async-start | bytes 2097152 | tf_op jit(solution)/shard_map/all_to_all | solution.py:60
  97.0 16.4 %all-to-all-done.1 = bf16[2,1024,256]{2,0,1:T(2,128)(2,1)S(1)} async-done(((bf16[2,1024,256]{2,0,1:T(2,128)(2,1)}), bf16[2,1024,256]{2,0,1:T(2,128)(2,1)S(1)}, u32[]{:S(2)}, u32[]{:S(2)}) %all-to-all-start.1) | async-done | bytes 1048608 | tf_op jit(solution)/shard_map/all_to_all | solution.py:60
  113.4 0.1 copy.28
  113.5 0.1 copy.29
  113.6 32.8 %while.14 = (s32[]{:T(128)}, f32[32,64,128]{2,1,0:T(8,128)S(1)}, s32[32,32]{1,0:T(8,128)}, bf16[32,64,256]{2,1,0:T(8,128)(2,1)S(1)}, s32[]{:T(128)}, /*index=5*/s32[]{:T(128)}, s32[]{:T(128)}, s32[]{:T(128)}) while((s32[]{:T(128)}, f32[32,64,128]{2,1,0:T(8,128)S(1)}, s32[32,32]{1,0:T(8,128)}, bf16[32,64,256]{2,1,0:T(8,128)(2,1)S(1)}, ...), condition=%wide.region_2.3_spmd.clone, body=%wide.region_1.2_spmd.clone.sunk | while | flops 541605888 | bytes 2362005 | solution.py:80
  113.6 0.7 constant_dynamic-slice_fusion.2
  114.3 0.1 copy.52
  114.4 0.1 iota_add_fusion.2
  114.5 3.2 %fusion.47 = f32[32,64,128]{2,1,0:T(8,128)S(1)} fusion(s32[4,32,128]{2,0,1:T(4,128)S(1)} %iota_add_fusion.2, f32[32,64,128]{2,1,0:T(8,128)S(1)} %get-tuple-element.193, pred[]{:T(512)S(6)} %compare.16, bf16[32,64,256]{2,1,0:T(8,128)(2,1)S(1)} %get-tuple-element.203, s32[]{:T(128)S(6)} %select_n.74), kind=kOutput, calls=%fused_computation.8.clone.1 | convolution fusion | flops 541589504 | bytes 2293765 | tf_op jit(solution)/shard_map/while/body/eval_jaxpr/jsv,jvra->rsa/dot_general | solution.py:75
  117.7 0.7 constant_dynamic-slice_fusion.2
  118.4 0.1 copy.52
  118.5 0.1 iota_add_fusion.2
  118.6 3.2 %fusion.47 = f32[32,64,128]{2,1,0:T(8,128)S(1)} fusion(s32[4,32,128]{2,0,1:T(4,128)S(1)} %iota_add_fusion.2, f32[32,64,128]{2,1,0:T(8,128)S(1)} %get-tuple-element.193, pred[]{:T(512)S(6)} %compare.16, bf16[32,64,256]{2,1,0:T(8,128)(2,1)S(1)} %get-tuple-element.203, s32[]{:T(128)S(6)} %select_n.74), kind=kOutput, calls=%fused_computation.8.clone.1 | convolution fusion | flops 541589504 | bytes 2293765 | tf_op jit(solution)/shard_map/while/body/eval_jaxpr/jsv,jvra->rsa/dot_general | solution.py:75
  121.8 0.7 constant_dynamic-slice_fusion.2
  122.5 0.1 copy.52
  122.6 0.1 iota_add_fusion.2
  122.7 3.2 %fusion.47 = f32[32,64,128]{2,1,0:T(8,128)S(1)} fusion(s32[4,32,128]{2,0,1:T(4,128)S(1)} %iota_add_fusion.2, f32[32,64,128]{2,1,0:T(8,128)S(1)} %get-tuple-element.193, pred[]{:T(512)S(6)} %compare.16, bf16[32,64,256]{2,1,0:T(8,128)(2,1)S(1)} %get-tuple-element.203, s32[]{:T(128)S(6)} %select_n.74), kind=kOutput, calls=%fused_computation.8.clone.1 | convolution fusion | flops 541589504 | bytes 2293765 | tf_op jit(solution)/shard_map/while/body/eval_jaxpr/jsv,jvra->rsa/dot_general | solution.py:75
  125.9 0.7 constant_dynamic-slice_fusion.2
  126.6 0.1 copy.52
  126.7 0.1 iota_add_fusion.2
  126.8 3.2 %fusion.47 = f32[32,64,128]{2,1,0:T(8,128)S(1)} fusion(s32[4,32,128]{2,0,1:T(4,128)S(1)} %iota_add_fusion.2, f32[32,64,128]{2,1,0:T(8,128)S(1)} %get-tuple-element.193, pred[]{:T(512)S(6)} %compare.16, bf16[32,64,256]{2,1,0:T(8,128)(2,1)S(1)} %get-tuple-element.203, s32[]{:T(128)S(6)} %select_n.74), kind=kOutput, calls=%fused_computation.8.clone.1 | convolution fusion | flops 541589504 | bytes 2293765 | tf_op jit(solution)/shard_map/while/body/eval_jaxpr/jsv,jvra->rsa/dot_general | solution.py:75
  130.0 0.7 constant_dynamic-slice_fusion.2
  130.7 0.1 copy.52
  130.8 0.1 iota_add_fusion.2
  130.9 3.2 %fusion.47 = f32[32,64,128]{2,1,0:T(8,128)S(1)} fusion(s32[4,32,128]{2,0,1:T(4,128)S(1)} %iota_add_fusion.2, f32[32,64,128]{2,1,0:T(8,128)S(1)} %get-tuple-element.193, pred[]{:T(512)S(6)} %compare.16, bf16[32,64,256]{2,1,0:T(8,128)(2,1)S(1)} %get-tuple-element.203, s32[]{:T(128)S(6)} %select_n.74), kind=kOutput, calls=%fused_computation.8.clone.1 | convolution fusion | flops 541589504 | bytes 2293765 | tf_op jit(solution)/shard_map/while/body/eval_jaxpr/jsv,jvra->rsa/dot_general | solution.py:75
  134.1 0.7 constant_dynamic-slice_fusion.2
  134.8 0.1 copy.52
  134.9 0.1 iota_add_fusion.2
  135.0 3.2 %fusion.47 = f32[32,64,128]{2,1,0:T(8,128)S(1)} fusion(s32[4,32,128]{2,0,1:T(4,128)S(1)} %iota_add_fusion.2, f32[32,64,128]{2,1,0:T(8,128)S(1)} %get-tuple-element.193, pred[]{:T(512)S(6)} %compare.16, bf16[32,64,256]{2,1,0:T(8,128)(2,1)S(1)} %get-tuple-element.203, s32[]{:T(128)S(6)} %select_n.74), kind=kOutput, calls=%fused_computation.8.clone.1 | convolution fusion | flops 541589504 | bytes 2293765 | tf_op jit(solution)/shard_map/while/body/eval_jaxpr/jsv,jvra->rsa/dot_general | solution.py:75
  138.2 0.7 constant_dynamic-slice_fusion.2
  138.9 0.1 copy.52
  139.0 0.1 iota_add_fusion.2
  139.1 3.2 %fusion.47 = f32[32,64,128]{2,1,0:T(8,128)S(1)} fusion(s32[4,32,128]{2,0,1:T(4,128)S(1)} %iota_add_fusion.2, f32[32,64,128]{2,1,0:T(8,128)S(1)} %get-tuple-element.193, pred[]{:T(512)S(6)} %compare.16, bf16[32,64,256]{2,1,0:T(8,128)(2,1)S(1)} %get-tuple-element.203, s32[]{:T(128)S(6)} %select_n.74), kind=kOutput, calls=%fused_computation.8.clone.1 | convolution fusion | flops 541589504 | bytes 2293765 | tf_op jit(solution)/shard_map/while/body/eval_jaxpr/jsv,jvra->rsa/dot_general | solution.py:75
  142.3 0.7 constant_dynamic-slice_fusion.2
  143.0 0.1 copy.52
  143.1 0.1 iota_add_fusion.2
  143.2 3.2 %fusion.47 = f32[32,64,128]{2,1,0:T(8,128)S(1)} fusion(s32[4,32,128]{2,0,1:T(4,128)S(1)} %iota_add_fusion.2, f32[32,64,128]{2,1,0:T(8,128)S(1)} %get-tuple-element.193, pred[]{:T(512)S(6)} %compare.16, bf16[32,64,256]{2,1,0:T(8,128)(2,1)S(1)} %get-tuple-element.203, s32[]{:T(128)S(6)} %select_n.74), kind=kOutput, calls=%fused_computation.8.clone.1 | convolution fusion | flops 541589504 | bytes 2293765 | tf_op jit(solution)/shard_map/while/body/eval_jaxpr/jsv,jvra->rsa/dot_general | solution.py:75
  146.4 0.0 copy-start
  146.4 0.1 multiply_convert_fusion
  146.5 14.4 %all_to_all.38 = bf16[8,4,64,128]{3,2,1,0:T(8,128)(2,1)S(1)} all-to-all(bf16[8,4,64,128]{3,2,1,0:T(8,128)(2,1)S(1)} %bitcast.70), channel_id=1, replica_groups=mesh['sub'=8,'beam'=16] {'sub'}, dimensions={0} | all-to-all | bytes 1048576 | tf_op jit(solution)/shard_map/all_to_all | solution.py:22
  160.9 0.7 convert_reduce_fusion
  161.6 0.0 copy-done
  (5 shorter events, 0.0 us)
Async XLA Ops:
  25.7 11.2 %copy-start.1 = (s32[1024]{0:T(1024)S(1)}, s32[1024]{0:T(1024)}, u32[]{:S(2)}) copy-start(s32[1024]{0:T(1024)} %param.8) | copy-start | bytes 12292
  25.7 41.5 %all-to-all-start = ((bf16[1,8,2,128,2,256]{5,1,4,2,0,3:T(8,128)(2,1)}), bf16[1,8,2,128,2,256]{5,1,4,2,0,3:T(8,128)(2,1)S(1)}, u32[]{:S(2)}, u32[]{:S(2)}) async-start(bf16[1,8,2,128,2,256]{5,1,4,2,0,3:T(8,128)(2,1)} %copy.23), calls=%async_computation | async-start | bytes 4194304 | tf_op jit(solution)/shard_map/all_to_all | solution.py:50
  93.3 20.1 %all-to-all-start.1 = ((bf16[2,1024,256]{2,0,1:T(2,128)(2,1)}), bf16[2,1024,256]{2,0,1:T(2,128)(2,1)S(1)}, u32[]{:S(2)}, u32[]{:S(2)}) async-start(bf16[2,1024,256]{2,0,1:T(2,128)(2,1)} %copy.27), calls=%async_computation.1 | async-start | bytes 2097152 | tf_op jit(solution)/shard_map/all_to_all | solution.py:60
  146.4 15.2 %copy-start = (bf16[32,64,256]{2,1,0:T(8,128)(2,1)}, bf16[32,64,256]{2,1,0:T(8,128)(2,1)S(1)}, u32[]{:S(2)}) copy-start(bf16[32,64,256]{2,1,0:T(8,128)(2,1)S(1)} %get-tuple-element.212) | copy-start | bytes 3145732
where the time goes:
time: 162 us
  matrix products  43.2 us (27%)
  waiting for transfers between devices  42.2 us (26%)
  local copies, waits for them, and re-layouts  30.9 us (19%)
  other arithmetic  15.1 us (9%)
  starting transfers between devices  14.8 us (9%)
  blocking collectives  14.4 us (9%)
    all_to_all x1, waiting for transfers between devices, on_device(): lax.all_to_all(direct_path, ('sub', 'beam'), split_axis=3, concat_axis=0,...  25.8 us
    dot_general x8, matrix products, add_block(): jnp.einsum('jsv,jvra->rsa', spectra_piece, channel_selector, preferred_el...  25.4 us
    all_to_all x1, waiting for transfers between devices, on_device(): lax.all_to_all(power, 'beam', split_axis=1, concat_axis=0, tiled=True)  16.4 us
    all_to_all x1, blocking collectives, sum_at_owner(): pieces = lax.all_to_all(cut_along(x, dim, devices), axis, 0, 0, tiled=True)  14.4 us
    all_to_all x1, starting transfers between devices, on_device(): lax.all_to_all(direct_path, ('sub', 'beam'), split_axis=3, concat_axis=0,...  11.2 us
    dot_general x1, matrix products, on_device(): jnp.einsum('ocin,afin->aocf', dft_table(), voltages, preferred_element_ty...  10.2 us
    another operation x2, other arithmetic  8.29 us
    gather x1, local copies, waits for them, and re-layouts, on_device(): by_antenna = jnp.take(spectra, inverse, axis=0)  7.9 us
  transfers between devices with their start and end apart: 2, of which 2 were waited for; matrix products, arithmetic and copies ran while one was open for 3% of the time, Pallas kernels for 0%

commit v1 on v0

v1 whole, which is shorter than its diff:
```python
import math

import numpy as np
import jax
import jax.numpy as jnp
from jax import lax
from jax.experimental import pallas as pl
from jax.experimental.pallas import tpu as pltpu
from jax.sharding import PartitionSpec as P

A = 1024
NFFT = 1024
C = 256
TRIALS = 32
OUT = 128
FR = 256
HALF = OUT // 2
ROWS = FR - HALF


def dft_table():
    sample = np.arange(NFFT)
    channel = np.arange(C)
    phase = (channel[:, None] * sample[None, :] % NFFT) * (2.0 * math.pi / NFFT)
    cosine = np.cos(phase) / math.sqrt(NFFT)
    sine = np.sin(phase) / math.sqrt(NFFT)
    real_row = np.stack([cosine, sine], axis=1)
    imag_row = np.stack([-sine, cosine], axis=1)
    return np.stack([real_row, imag_row], axis=0).astype(jnp.bfloat16)


def beam_kernel(map_ref, spectra_ref, weight_ref, power_ref, ordered_ref):
    @pl.when(pl.program_id(1) == 0)
    def _():
        rows = lax.broadcasted_iota(jnp.int32, (A, A), 0)
        place = jnp.where(rows == map_ref[...], 1.0, 0.0).astype(jnp.bfloat16)
        for part in range(2):
            piece = spectra_ref[:, part].reshape(A, FR)
            ordered_ref[:, part * FR : (part + 1) * FR] = jnp.dot(
                place, piece, preferred_element_type=jnp.float32
            ).astype(jnp.bfloat16)

    data = ordered_ref[...]
    by_re = jnp.dot(weight_ref[0, 0], data, preferred_element_type=jnp.float32)
    by_im = jnp.dot(weight_ref[0, 1], data, preferred_element_type=jnp.float32)
    beam_re = by_re[:, :FR] - by_im[:, FR:]
    beam_im = by_re[:, FR:] + by_im[:, :FR]
    power = (beam_re * beam_re + beam_im * beam_im).astype(jnp.bfloat16)
    power_ref[...] = power.reshape(power_ref.shape)


def form_beams(antenna_map, spectra, weights, beam_count):
    owned, beams = weights.shape[0], weights.shape[2]
    block = 256
    width = beams // beam_count
    per_block = block // width
    return pl.pallas_call(
        beam_kernel,
        grid=(owned, beams // block),
        in_specs=[
            pl.BlockSpec((1, A), lambda k, b: (0, 0)),
            pl.BlockSpec((spectra.shape[0], 2, spectra.shape[2], FR), lambda k, b: (0, k, 0, 0)),
            pl.BlockSpec((1, 2, block, A), lambda k, b: (k, 0, b, 0)),
        ],
        out_specs=pl.BlockSpec((per_block, 1, width, FR), lambda k, b: (b, k, 0, 0)),
        out_shape=jax.ShapeDtypeStruct((beam_count, owned, width, FR), jnp.bfloat16),
        scratch_shapes=[pltpu.VMEM((A, 2 * FR), jnp.bfloat16)],
        compiler_params=pltpu.CompilerParams(vmem_limit_bytes=32 << 20),
    )(antenna_map.reshape(1, A), spectra, weights)


def dedisperse_kernel(delay_ref, power_ref, out_ref, turned_ref):
    channels = power_ref.shape[0]

    def turn(c, carry):
        power = power_ref[c].astype(jnp.float32)
        both = jnp.concatenate([power, pltpu.roll(power, FR - HALF, 1)], axis=0)
        turned_ref[pl.ds(pl.multiple_of(c * ROWS, 8), ROWS), :] = both.T[:ROWS]
        return carry

    lax.fori_loop(0, channels, turn, 0)

    def trial(t, carry):
        total = turned_ref[pl.ds(delay_ref[0, t], HALF), :]
        for c in range(1, channels):
            total = total + turned_ref[pl.ds(c * ROWS + delay_ref[c, t], HALF), :]
        out_ref[t] = (total * (1.0 / C)).astype(jnp.bfloat16)
        return carry

    lax.fori_loop(0, TRIALS, trial, 0)


def dedisperse(filterbank, delays):
    channels, beams = filterbank.shape[:2]
    return pl.pallas_call(
        dedisperse_kernel,
        in_specs=[
            pl.BlockSpec(memory_space=pltpu.SMEM),
            pl.BlockSpec(memory_space=pltpu.VMEM),
        ],
        out_specs=pl.BlockSpec(memory_space=pltpu.VMEM),
        out_shape=jax.ShapeDtypeStruct((TRIALS, HALF, 2 * beams), jnp.bfloat16),
        scratch_shapes=[pltpu.VMEM((channels * ROWS, 2 * beams), jnp.float32)],
        compiler_params=pltpu.CompilerParams(vmem_limit_bytes=32 << 20),
    )(delays, filterbank)


def sum_kernel(pieces_ref, out_ref):
    beams = out_ref.shape[1]
    for t in range(out_ref.shape[0]):
        total = pieces_ref[0, t].astype(jnp.float32)
        for s in range(1, pieces_ref.shape[0]):
            total = total + pieces_ref[s, t].astype(jnp.float32)
        turned = total.T
        out_ref[t] = jnp.concatenate([turned[:beams], turned[beams:]], axis=1)


def sum_pieces(pieces):
    beams = pieces.shape[3] // 2
    return pl.pallas_call(
        sum_kernel,
        out_shape=jax.ShapeDtypeStruct((pieces.shape[1], beams, OUT), jnp.float32),
    )(pieces)


def on_device(voltages, weights, antenna_map, delays):
    antennas = voltages.shape[0]
    subband_count = lax.axis_size("sub")
    beam_count = lax.axis_size("beam")
    devices = subband_count * beam_count
    owned = C // devices
    table = jnp.asarray(dft_table()).reshape(2, devices, owned, 2, NFFT)
    spectra = jnp.einsum(
        "odkin,afin->dkoaf", table, voltages, preferred_element_type=jnp.float32
    ).astype(jnp.bfloat16)
    spectra = spectra.reshape(devices, owned * 2, antennas, FR)
    moved = lax.all_to_all(spectra, ("sub", "beam"), 0, 0, tiled=True)
    power = form_beams(antenna_map, moved, weights, beam_count)
    filterbank = lax.all_to_all(power, "beam", 0, 0, tiled=True)
    filterbank = filterbank.reshape(beam_count * owned, -1, FR)
    partial = dedisperse(filterbank, delays)
    pieces = partial.reshape(subband_count, TRIALS // subband_count, *partial.shape[1:])
    series = sum_pieces(lax.all_to_all(pieces, "sub", 0, 0, tiled=True))
    return (filterbank, series)


def solution(mesh):
    placed = (
        P(("sub", "beam"), None, None, None),
        P(("sub", "beam"), None, None, None),
        P(),
        P("sub", None),
    )
    return jax.shard_map(
        on_device,
        mesh=mesh,
        in_specs=placed,
        out_specs=(P("sub", "beam", None), P("sub", "beam", None)),
        check_vma=False,
    )
```

time: 162 us -> 106 us (0.65)
  blocking collectives: 14.4 us -> 74.6 us
  waiting for transfers between devices: 42.2 us -> 0 us
  matrix products: 43.2 us -> 8.68 us
  local copies, waits for them, and re-layouts: 30.9 us -> 2.17 us
  Pallas kernels: 0 us -> 19.3 us
  other arithmetic: 15.1 us -> 0 us
  starting transfers between devices: 14.8 us -> 0 us
    all_to_all x1 -> x3, blocking collectives: 14.4 us -> 74.6 us  [the longest x1 41.3 us: on_device(): moved = lax.all_to_all(spectra, ('sub', 'beam'), 0, 0, tiled=True)]
    all_to_all x2 -> x0, waiting for transfers between devices: 42.2 us -> none  [the longest x1 25.8 us: on_device(): lax.all_to_all(direct_path, ('sub', 'beam'), split_axis=3, concat_axis=0,...]
    dot_general x10 -> x1, matrix products: 43.2 us -> 8.68 us  [on_device(): jnp.einsum('odkin,afin->dkoaf', table, voltages, preferred_element_type=j...]
    pallas_call x0 -> x3, Pallas kernels: none -> 19.3 us  [the longest x1 9.13 us: form_beams(): pl.pallas_call(beam_kernel, grid=(owned, beams // block), in_specs=[pl.Bl...]
    all_to_all x2 -> x0, starting transfers between devices: 14.8 us -> none  [the longest x1 11.2 us: on_device(): lax.all_to_all(direct_path, ('sub', 'beam'), split_axis=3, concat_axis=0,...]
    reshape x3 -> x0, local copies, waits for them, and re-layouts: 9.81 us -> none  [the longest x2 6.32 us: on_device(): local_spectra.reshape(1, antenna_per_device, 2, subband_count * beam_coun...]
    another operation x3 -> x0, other arithmetic: 8.48 us -> none
    gather x1 -> x0, local copies, waits for them, and re-layouts: 7.9 us -> none  [on_device(): by_antenna = jnp.take(spectra, inverse, axis=0)]
  transfers between devices with their start and end apart: 2 -> 0, of which waited for: 2 -> 0; matrix products, arithmetic and copies ran while one was open for 3% -> 0% of each run, Pallas kernels for 0% -> 0%
where the time goes in v1:
time: 106 us; the launch traced here: 105 us
  blocking collectives  74.6 us (70%)
  Pallas kernels  19.3 us (18%)
  matrix products  8.68 us (8%)
  local copies, waits for them, and re-layouts  2.17 us (2%)
    all_to_all x1, blocking collectives, on_device(): moved = lax.all_to_all(spectra, ('sub', 'beam'), 0, 0, tiled=True)  41.3 us
    all_to_all x1, blocking collectives, on_device(): filterbank = lax.all_to_all(power, 'beam', 0, 0, tiled=True)  19.1 us
    all_to_all x1, blocking collectives, on_device(): series = sum_pieces(lax.all_to_all(pieces, 'sub', 0, 0, tiled=True))  14.2 us
    pallas_call x1, Pallas kernels, form_beams(): pl.pallas_call(beam_kernel, grid=(owned, beams // block), in_specs=[pl.Bl...  9.13 us
    dot_general x1, matrix products, on_device(): jnp.einsum('odkin,afin->dkoaf', table, voltages, preferred_element_type=j...  8.68 us
    pallas_call x1, Pallas kernels, dedisperse(): pl.pallas_call(dedisperse_kernel, in_specs=[pl.BlockSpec(memory_space=plt...  8.21 us

profile of v1, /device:TPU:0, one launch (start us, length us, event | category | flops | bytes accessed | tf_op | source)
XLA Modules:
  0.0 105.4 jit_solution(17133767573449598575)
XLA Ops:
  0.6 0.0 copy-start.2
  0.6 8.7 %fusion.4 = bf16[128,2,2,8,256]{4,0,3,1,2:T(8,128)(2,1)S(1)} fusion(bf16[2,128,2,2,1024,1]{4,1,3,5,2,0:T(8,128)(2,1)} %constant.6, bf16[8,256,2,1024,1,1]{3,2,1,0,5,4:T(2,128)(2,1)} %bitcast.21), kind=kOutput, calls=%fused_computation.3 | convolution fusion | flops 4296015872 | bytes 12582912 | tf_op jit(solution)/shard_map/odkin,afin->dkoaf/dot_general | solution.py:133
  9.3 0.0 copy-start
  9.3 1.2 %copy.8 = bf16[128,2,2,8,256]{4,3,2,1,0:T(8,128)(2,1)S(1)} copy(bf16[128,2,2,8,256]{4,0,3,1,2:T(8,128)(2,1)S(1)} %fusion.4) | data formatting | bytes 4194304 | tf_op jit(solution)/shard_map/convert_element_type | solution.py:135
  10.5 41.3 %all_to_all.15.spectra_ref = bf16[128,4,8,256]{3,2,1,0:T(8,128)(2,1)S(1)} all-to-all(bf16[128,4,8,256]{3,2,1,0:T(8,128)(2,1)S(1)} %bitcast.20), channel_id=1, replica_groups=mesh['sub'=8,'beam'=16] {'sub','beam'}, dimensions={0} | all-to-all | bytes 4194304 | tf_op jit(solution)/shard_map/all_to_all | solution.py:137
  51.8 0.0 copy-done.2
  51.8 0.0 copy-done
  51.8 9.1 %shard_map.68 = bf16[16,2,64,256]{3,2,1,0:T(8,128)(2,1)S(1)} custom-call(s32[1,1024]{1,0:T(1,128)S(1)} %bitcast.19, bf16[128,4,8,256]{3,2,1,0:T(8,128)(2,1)S(1)} %all_to_all.15.spectra_ref, bf16[2,2,1024,1024]{3,2,1,0:T(8,128)(2,1)S(1)} %copy-done), custom_call_target="tpu_custom_call" | custom-call | tf_op jit(solution)/shard_map/pallas_call | solution.py:57
  61.0 0.0 copy-start.1
  61.0 19.1 %all_to_all.16 = bf16[16,2,64,256]{3,2,1,0:T(8,128)(2,1)S(1)} all-to-all(bf16[16,2,64,256]{3,2,1,0:T(8,128)(2,1)S(1)} %shard_map.68), channel_id=1, replica_groups=mesh['sub'=8,'beam'=16] {'beam'}, dimensions={0} | all-to-all | bytes 2097152 | tf_op jit(solution)/shard_map/all_to_all | solution.py:139
  80.1 0.0 copy-done.1
  80.1 8.2 %shard_map.69 = bf16[32,64,128]{2,1,0:T(8,128)(2,1)S(1)} custom-call(s32[32,32]{1,0:T(8,128)S(1)} %copy-done.1, bf16[32,64,256]{2,1,0:T(8,128)(2,1)S(1)} %bitcast.16), custom_call_target="tpu_custom_call" | custom-call | tf_op jit(solution)/shard_map/pallas_call | solution.py:95
  88.3 14.2 %all_to_all.17.pieces_ref = bf16[8,4,64,128]{3,2,1,0:T(8,128)(2,1)} all-to-all(bf16[8,4,64,128]{3,2,1,0:T(8,128)(2,1)S(1)} %bitcast.18), channel_id=1, replica_groups=mesh['sub'=8,'beam'=16] {'sub'}, dimensions={0} | all-to-all | bytes 1048576 | tf_op jit(solution)/shard_map/all_to_all | solution.py:143
  102.5 1.9 %shard_map.70 = f32[4,64,128]{2,1,0:T(8,128)} custom-call(bf16[8,4,64,128]{3,2,1,0:T(8,128)(2,1)} %all_to_all.17.pieces_ref), custom_call_target="tpu_custom_call" | custom-call | tf_op jit(solution)/shard_map/pallas_call | solution.py:120
  104.4 1.0 copy.21
Async XLA Ops:
  0.6 51.2 %copy-start.2 = (s32[1024]{0:T(1024)S(1)}, s32[1024]{0:T(1024)}, u32[]{:S(2)}) copy-start(s32[1024]{0:T(1024)} %param.7) | copy-start | bytes 12292
  9.3 42.5 %copy-start = (bf16[2,2,1024,1024]{3,2,1,0:T(8,128)(2,1)S(1)}, bf16[2,2,1024,1024]{3,2,1,0:T(8,128)(2,1)}, u32[]{:S(2)}) copy-start(bf16[2,2,1024,1024]{3,2,1,0:T(8,128)(2,1)} %weight_ref.1) | copy-start | bytes 25165828
  61.0 19.1 %copy-start.1 = (s32[32,32]{1,0:T(8,128)S(1)}, s32[32,32]{1,0:T(8,128)}, u32[]{:S(2)}) copy-start(s32[32,32]{1,0:T(8,128)} %delay_ref.1) | copy-start | bytes 12292

commit v2 on v1

v2 whole, which is shorter than its diff:
```python
import math

import numpy as np
import jax
import jax.numpy as jnp
from jax import lax
from jax.experimental import pallas as pl
from jax.experimental.pallas import tpu as pltpu
from jax.sharding import PartitionSpec as P

A = 1024
NFFT = 1024
C = 256
TRIALS = 32
OUT = 128
FR = 256
HALF = OUT // 2
ROWS = FR - HALF


def dft_table():
    sample = np.arange(NFFT // 4)
    channel = np.arange(C)
    phase = (channel[:, None] * sample[None, :] % NFFT) * (2.0 * math.pi / NFFT)
    cosine = np.cos(phase) / math.sqrt(NFFT)
    sine = np.sin(phase) / math.sqrt(NFFT)
    real_row = np.concatenate([cosine, sine], axis=1)
    imag_row = np.concatenate([-sine, cosine], axis=1)
    rows = np.stack([real_row, imag_row], axis=0)
    rows = rows.reshape(2, C // 4, 4, NFFT // 2).transpose(2, 0, 1, 3)
    return rows.reshape(4, C // 2, NFFT // 2).astype(jnp.bfloat16)


PITCH = 20
SPAN = 65
FRAMES = 16
PAIR = 2


def mix_frames(sample_ref, wide_ref, mixed_ref, row, first):
    for f in range(FRAMES):
        start = row + (first + f) * 16
        wide_ref[PITCH * (first + f) : PITCH * (first + f) + 16, :] = sample_ref[start : start + 16, :].astype(jnp.float32)

    def pick(block, part):
        return wide_ref[pl.ds(PITCH * first + 2 * block + part, FRAMES, stride=PITCH), :]

    for half in range(2):
        re = [pick(2 * j + half, 0) for j in range(4)]
        im = [pick(2 * j + half, 1) for j in range(4)]
        add_re, sub_re = re[0] + re[2], re[0] - re[2]
        add_im, sub_im = im[0] + im[2], im[0] - im[2]
        odd_add_re, odd_sub_re = re[1] + re[3], re[1] - re[3]
        odd_add_im, odd_sub_im = im[1] + im[3], im[1] - im[3]
        mixed = (
            (add_re + odd_add_re, add_im + odd_add_im),
            (sub_re + odd_sub_im, sub_im - odd_sub_re),
            (add_re - odd_add_re, add_im - odd_add_im),
            (sub_re - odd_sub_im, sub_im + odd_sub_re),
        )
        for r in range(4):
            for part in range(2):
                lane = part * 256 + half * 128
                mixed_ref[r, first : first + FRAMES, lane : lane + 128] = mixed[r][part].astype(jnp.bfloat16)


def transform(table_ref, mixed_ref, done_ref, antenna):
    groups = C // 4
    for r in range(4):
        got = lax.dot_general(
            table_ref[r],
            mixed_ref[r],
            (((1,), (1,)), ((), ())),
            preferred_element_type=jnp.float32,
        )
        for part in range(2):
            start = r * 16 + part * 8 + antenna
            for side in range(2):
                done_ref[side, pl.ds(start, groups, stride=SPAN), :] = got[
                    part * groups : part * groups + groups, side * 128 : side * 128 + 128
                ]


def channel_kernel(table_ref, sample_ref, out_ref, wide_a, wide_b, mixed_a, mixed_b, done_ref):
    antenna = pl.program_id(0) * PAIR
    last = PAIR * (pl.num_programs(0) - 1)
    before = jnp.where(antenna == 0, last + 1, antenna - 1)

    @pl.when(antenna == 0)
    def _():
        mixed_b[...] = jnp.zeros(mixed_b.shape, mixed_b.dtype)

    transform(table_ref, mixed_b, done_ref, before)
    for first in range(0, FR, FRAMES):
        mix_frames(sample_ref, wide_a, mixed_a, 0, first)
    transform(table_ref, mixed_a, done_ref, antenna)
    for first in range(0, FR, FRAMES):
        mix_frames(sample_ref, wide_b, mixed_b, FR * 16, first)

    @pl.when(antenna == last)
    def _():
        transform(table_ref, mixed_b, done_ref, antenna + 1)
        for side in range(2):
            lanes = slice(side * 128, side * 128 + 128)
            for q in range(C // 4):
                block = done_ref[side, SPAN * q : SPAN * q + 64, :]
                out_ref[8 * q : 8 * q + 8, :, lanes] = block.reshape(8, 8, 128).astype(jnp.bfloat16)


def channelize(voltages):
    antennas = voltages.shape[0]
    rows = FR * 16
    flat = voltages.reshape(antennas, FR, 2, 8, 128).transpose(0, 1, 3, 2, 4).reshape(antennas * rows, 128)
    flat = pltpu.with_memory_space_constraint(flat, pltpu.HBM)
    table = jnp.asarray(dft_table())
    mixed = pltpu.VMEM((4, FR, NFFT // 2), jnp.bfloat16)
    wide = pltpu.VMEM((FR * PITCH, 128), jnp.float32)
    return pl.pallas_call(
        channel_kernel,
        grid=(antennas // PAIR,),
        in_specs=[
            pl.BlockSpec(table.shape, lambda a: (0, 0, 0)),
            pl.BlockSpec((PAIR * rows, 128), lambda a: (a, 0)),
        ],
        out_specs=pl.BlockSpec((2 * C, antennas, FR), lambda a: (0, 0, 0)),
        out_shape=pltpu.HBM((2 * C, antennas, FR), jnp.bfloat16),
        scratch_shapes=[wide, wide, mixed, mixed, pltpu.VMEM((2, C // 4 * SPAN, 128), jnp.float32)],
        compiler_params=pltpu.CompilerParams(vmem_limit_bytes=32 << 20),
    )(table, flat)


def beam_kernel(spectra_ref, weight_ref, power_ref, data_ref):
    @pl.when(pl.program_id(1) == 0)
    def _():
        for part in range(2):
            data_ref[:, part * FR : (part + 1) * FR] = spectra_ref[:, part].reshape(A, FR)

    block = 256
    width = power_ref.shape[2]
    for first in range(0, weight_ref.shape[2], block):
        both = weight_ref[0, :, first : first + block].reshape(2 * block, A)
        made = jnp.dot(both, data_ref[...], preferred_element_type=jnp.float32)
        beam_re = made[:block, :FR] - made[block:, FR:]
        beam_im = made[:block, FR:] + made[block:, :FR]
        power = (beam_re * beam_re + beam_im * beam_im).astype(jnp.bfloat16)
        power_ref[first // width : (first + block) // width, 0] = power.reshape(block // width, width, FR)


def order_kernel(map_ref, weight_ref, out_ref, place_ref):
    @pl.when((pl.program_id(0) == 0) & (pl.program_id(1) == 0))
    def _():
        rows = lax.broadcasted_iota(jnp.int32, (A, A), 0)
        place_ref[...] = jnp.where(rows == map_ref[...], 1.0, 0.0).astype(jnp.bfloat16)

    both = weight_ref[0].reshape(-1, A)
    moved = jnp.dot(both, place_ref[...], preferred_element_type=jnp.float32)
    out_ref[0] = moved.astype(jnp.bfloat16).reshape(out_ref.shape[1:])


def order_weights(antenna_map, weights):
    owned, beams = weights.shape[0], weights.shape[2]
    block = 256
    spec = pl.BlockSpec((1, 2, block, A), lambda k, b: (k, 0, b, 0))
    return pl.pallas_call(
        order_kernel,
        grid=(owned, beams // block),
        in_specs=[pl.BlockSpec((1, A), lambda k, b: (0, 0)), spec],
        out_specs=spec,
        out_shape=pltpu.HBM(weights.shape, jnp.bfloat16),
        scratch_shapes=[pltpu.VMEM((A, A), jnp.bfloat16)],
        compiler_params=pltpu.CompilerParams(vmem_limit_bytes=16 << 20),
    )(antenna_map.reshape(1, A), pltpu.with_memory_space_constraint(weights, pltpu.HBM))


def form_beams(spectra, weights, beam_count):
    owned, beams = weights.shape[0], weights.shape[2]
    block = 1024
    width = beams // beam_count
    per_block = block // width
    return pl.pallas_call(
        beam_kernel,
        grid=(owned, beams // block),
        in_specs=[
            pl.BlockSpec((spectra.shape[0], 2, spectra.shape[2], FR), lambda k, b: (0, k, 0, 0)),
            pl.BlockSpec((1, 2, block, A), lambda k, b: (k, 0, b, 0)),
        ],
        out_specs=pl.BlockSpec((per_block, 1, width, FR), lambda k, b: (b, k, 0, 0)),
        out_shape=jax.ShapeDtypeStruct((beam_count, owned, width, FR), jnp.bfloat16),
        scratch_shapes=[pltpu.VMEM((A, 2 * FR), jnp.bfloat16)],
        compiler_params=pltpu.CompilerParams(vmem_limit_bytes=32 << 20),
    )(spectra, pltpu.with_memory_space_constraint(weights, pltpu.HBM))


def dedisperse_kernel(delay_ref, power_ref, out_ref, kept_ref, turned_ref, sem):
    channels, beams = power_ref.shape[:2]
    keep = pltpu.make_async_copy(power_ref, kept_ref, sem)
    keep.start()
    rows = lax.broadcasted_iota(jnp.int32, (ROWS, FR), 0)
    lanes = lax.broadcasted_iota(jnp.int32, (ROWS, FR), 1)
    unit = jnp.where(rows == lanes, 1.0, 0.0).astype(jnp.bfloat16)

    for pair in range(channels // 2):
        parts = []
        for c in range(2):
            power = power_ref[2 * pair + c]
            parts += [power, jnp.concatenate([power[:, HALF:], power[:, :HALF]], axis=1)]
        both = lax.dot_general(
            unit,
            jnp.concatenate(parts, axis=0),
            (((1,), (1,)), ((), ())),
            preferred_element_type=jnp.float32,
        )
        for c in range(2):
            start = (2 * pair + c) * ROWS
            turned_ref[start : start + ROWS, :] = both[:, c * 2 * beams : (c + 1) * 2 * beams]

    def trial(pair, carry):
        for t in (2 * pair, 2 * pair + 1):
            total = turned_ref[pl.ds(delay_ref[0, t], HALF), :]
            for c in range(1, channels):
                total = total + turned_ref[pl.ds(c * ROWS + delay_ref[c, t], HALF), :]
            out_ref[t] = (total * (1.0 / C)).astype(jnp.bfloat16)
        return carry

    lax.fori_loop(0, TRIALS // 2, trial, 0)
    keep.wait()


def dedisperse(filterbank, delays):
    channels, beams = filterbank.shape[:2]
    return pl.pallas_call(
        dedisperse_kernel,
        in_specs=[
            pl.BlockSpec(memory_space=pltpu.SMEM),
            pl.BlockSpec(memory_space=pltpu.VMEM),
        ],
        out_specs=(
            pl.BlockSpec(memory_space=pltpu.VMEM),
            pl.BlockSpec(memory_space=pltpu.HBM),
        ),
        out_shape=(
            jax.ShapeDtypeStruct((TRIALS, HALF, 2 * beams), jnp.bfloat16),
            jax.ShapeDtypeStruct(filterbank.shape, filterbank.dtype),
        ),
        scratch_shapes=[
            pltpu.VMEM((channels * ROWS, 2 * beams), jnp.float32),
            pltpu.SemaphoreType.DMA,
        ],
        compiler_params=pltpu.CompilerParams(vmem_limit_bytes=16 << 20),
    )(delays, filterbank)


def sum_kernel(pieces_ref, out_ref):
    beams = out_ref.shape[1]
    for t in range(out_ref.shape[0]):
        total = pieces_ref[0, t].astype(jnp.float32)
        for s in range(1, pieces_ref.shape[0]):
            total = total + pieces_ref[s, t].astype(jnp.float32)
        turned = total.T
        out_ref[t] = jnp.concatenate([turned[:beams], turned[beams:]], axis=1)


def sum_pieces(pieces):
    beams = pieces.shape[3] // 2
    return pl.pallas_call(
        sum_kernel,
        out_shape=jax.ShapeDtypeStruct((pieces.shape[1], beams, OUT), jnp.float32),
    )(pieces)


def on_device(voltages, weights, antenna_map, delays):
    subband_count = lax.axis_size("sub")
    beam_count = lax.axis_size("beam")
    devices = subband_count * beam_count
    owned = C // devices
    spectra = channelize(voltages)
    spectra = spectra.reshape(devices, owned * 2, voltages.shape[0], FR)
    moved = lax.all_to_all(spectra, ("sub", "beam"), 0, 0, tiled=True)
    ordered = order_weights(antenna_map, weights)
    power = form_beams(moved, ordered, beam_count)
    filterbank = lax.all_to_all(power, "beam", 0, 0, tiled=True)
    filterbank = filterbank.reshape(beam_count * owned, -1, FR)
    partial, filterbank = dedisperse(filterbank, delays)
    pieces = partial.reshape(subband_count, TRIALS // subband_count, *partial.shape[1:])
    series = sum_pieces(lax.all_to_all(pieces, "sub", 0, 0, tiled=True))
    return (filterbank, series)


def solution(mesh):
    placed = (
        P(("sub", "beam"), None, None, None),
        P(("sub", "beam"), None, None, None),
        P(),
        P("sub", None),
    )
    return jax.shard_map(
        on_device,
        mesh=mesh,
        in_specs=placed,
        out_specs=(P("sub", "beam", None), P("sub", "beam", None)),
        check_vma=False,
    )
```

time: 106 us -> 100 us (0.943)
  blocking collectives: 74.6 us -> 33.3 us
  Pallas kernels: 19.3 us -> 36.9 us
  waiting for transfers between devices: 0 us -> 16.3 us
  starting transfers between devices: 0 us -> 11.2 us
  matrix products: 8.68 us -> 0 us
  local copies, waits for them, and re-layouts: 2.17 us -> 1.04 us
    all_to_all x1 -> x0, blocking collectives: 41.3 us -> none  [on_device(): moved = lax.all_to_all(spectra, ('sub', 'beam'), 0, 0, tiled=True)]
    pallas_call x0 -> x2, Pallas kernels: none -> 23.7 us  [the longest x1 14 us: order_weights(): pl.pallas_call(order_kernel, grid=(owned, beams // block), in_specs=[pl.B...]
    all_to_all x0 -> x1, waiting for transfers between devices: none -> 16.3 us  [on_device(): moved = lax.all_to_all(spectra, ('sub', 'beam'), 0, 0, tiled=True)]
    all_to_all x0 -> x1, starting transfers between devices: none -> 11.2 us  [on_device(): moved = lax.all_to_all(spectra, ('sub', 'beam'), 0, 0, tiled=True)]
    dot_general x1 -> x0, matrix products: 8.68 us -> none  [on_device(): jnp.einsum('odkin,afin->dkoaf', table, voltages, preferred_element_type=j...]
    pallas_call x1, Pallas kernels: 8.21 us -> 4.12 us  [dedisperse(): pl.pallas_call(dedisperse_kernel, in_specs=[pl.BlockSpec(memory_space=plt...]
    pallas_call x1, Pallas kernels: 9.13 us -> 7.11 us  [form_beams(): pl.pallas_call(beam_kernel, grid=(owned, beams // block), in_specs=[pl.Bl...]
    convert_element_type x1 -> x0, local copies, waits for them, and re-layouts: 1.19 us -> none  [on_device(): spectra = jnp.einsum('odkin,afin->dkoaf', table, voltages, preferred_elem...]
  transfers between devices with their start and end apart: 0 -> 1, of which waited for: 0 -> 1; matrix products, arithmetic and copies ran while one was open for 0% -> 0% of each run, Pallas kernels for 0% -> 14%
where the time goes in v2:
time: 100 us; the launch traced here: 99.4 us
  Pallas kernels  36.9 us (37%)
  blocking collectives  33.3 us (33%)
  waiting for transfers between devices  16.3 us (16%)
  starting transfers between devices  11.2 us (11%)
  local copies, waits for them, and re-layouts  1.04 us (1%)
    all_to_all x1, blocking collectives, on_device(): filterbank = lax.all_to_all(power, 'beam', 0, 0, tiled=True)  19.1 us
    all_to_all x1, waiting for transfers between devices, on_device(): moved = lax.all_to_all(spectra, ('sub', 'beam'), 0, 0, tiled=True)  16.3 us
    all_to_all x1, blocking collectives, on_device(): series = sum_pieces(lax.all_to_all(pieces, 'sub', 0, 0, tiled=True))  14.2 us
    pallas_call x1, Pallas kernels, order_weights(): pl.pallas_call(order_kernel, grid=(owned, beams // block), in_specs=[pl.B...  14 us
    all_to_all x1, starting transfers between devices, on_device(): moved = lax.all_to_all(spectra, ('sub', 'beam'), 0, 0, tiled=True)  11.2 us
    pallas_call x1, Pallas kernels, channelize(): pl.pallas_call(channel_kernel, grid=(antennas // PAIR,), in_specs=[pl.Blo...  9.69 us
    pallas_call x1, Pallas kernels, form_beams(): pl.pallas_call(beam_kernel, grid=(owned, beams // block), in_specs=[pl.Bl...  7.11 us
    pallas_call x1, Pallas kernels, dedisperse(): pl.pallas_call(dedisperse_kernel, in_specs=[pl.BlockSpec(memory_space=plt...  4.12 us
  transfers between devices with their start and end apart: 1, of which 1 were waited for; matrix products, arithmetic and copies ran while one was open for 0% of the time, Pallas kernels for 14%

profile of v2, /device:TPU:0, one launch (start us, length us, event | category | flops | bytes accessed | tf_op | source)
XLA Modules:
  0.0 99.4 jit_solution(2142847046823350931)
XLA Ops:
  0.6 0.0 copy-start
  0.6 1.0 %copy-done = bf16[4,128,512]{2,1,0:T(8,128)(2,1)S(1)} copy-done((bf16[4,128,512]{2,1,0:T(8,128)(2,1)S(1)}, bf16[4,128,512]{2,1,0:T(8,128)(2,1)}, u32[]{:S(2)}) %copy-start) | copy-done | bytes 524312
  1.7 0.0 copy-start.2
  1.7 9.7 %shard_map.68 = bf16[512,8,256]{2,1,0:T(8,128)(2,1)} custom-call(bf16[4,128,512]{2,1,0:T(8,128)(2,1)S(1)} %copy-done, bf16[32768,128]{1,0:T(8,128)(2,1)} %bitcast.12), custom_call_target="tpu_custom_call" | custom-call | tf_op jit(solution)/shard_map/pallas_call | solution.py:118
  11.4 11.2 %all-to-all-start = ((bf16[128,4,8,256]{3,2,1,0:T(8,128)(2,1)}), bf16[128,4,8,256]{3,2,1,0:T(8,128)(2,1)S(1)}, u32[]{:S(2)}, u32[]{:S(2)}) async-start(bf16[128,4,8,256]{3,2,1,0:T(8,128)(2,1)} %bitcast.13), calls=%async_computation | async-start | bytes 4194304 | tf_op jit(solution)/shard_map/all_to_all | solution.py:278
  22.6 0.0 copy-done.2
  22.6 14.0 %shard_map.69.weight_ref = bf16[2,2,1024,1024]{3,2,1,0:T(8,128)(2,1)} custom-call(s32[1,1024]{1,0:T(1,128)S(1)} %bitcast.11, bf16[2,2,1024,1024]{3,2,1,0:T(8,128)(2,1)} %weight_ref.1), custom_call_target="tpu_custom_call" | custom-call | tf_op jit(solution)/shard_map/pallas_call | solution.py:164
  36.6 0.0 copy-start.1
  36.6 16.3 %all-to-all-done.spectra_ref = bf16[128,4,8,256]{3,2,1,0:T(8,128)(2,1)S(1)} async-done(((bf16[128,4,8,256]{3,2,1,0:T(8,128)(2,1)}), bf16[128,4,8,256]{3,2,1,0:T(8,128)(2,1)S(1)}, u32[]{:S(2)}, u32[]{:S(2)}) %all-to-all-start) | async-done | bytes 2097184 | tf_op jit(solution)/shard_map/all_to_all | solution.py:278
  52.9 7.1 %shard_map.70 = bf16[16,2,64,256]{3,2,1,0:T(8,128)(2,1)S(1)} custom-call(bf16[128,4,8,256]{3,2,1,0:T(8,128)(2,1)S(1)} %all-to-all-done.spectra_ref, bf16[2,2,1024,1024]{3,2,1,0:T(8,128)(2,1)} %shard_map.69.weight_ref), custom_call_target="tpu_custom_call" | custom-call | tf_op jit(solution)/shard_map/pallas_call | solution.py:180
  60.0 19.1 %all_to_all.15 = bf16[16,2,64,256]{3,2,1,0:T(8,128)(2,1)S(1)} all-to-all(bf16[16,2,64,256]{3,2,1,0:T(8,128)(2,1)S(1)} %shard_map.70), channel_id=1, replica_groups=mesh['sub'=8,'beam'=16] {'beam'}, dimensions={0} | all-to-all | bytes 2097152 | tf_op jit(solution)/shard_map/all_to_all | solution.py:281
  79.1 0.0 copy-done.1
  79.1 4.1 %shard_map.71 = (bf16[32,64,128]{2,1,0:T(8,128)(2,1)S(1)}, bf16[32,64,256]{2,1,0:T(8,128)(2,1)}) custom-call(s32[32,32]{1,0:T(8,128)S(1)} %copy-done.1, bf16[32,64,256]{2,1,0:T(8,128)(2,1)S(1)} %bitcast.9), custom_call_target="tpu_custom_call" | custom-call | tf_op jit(solution)/shard_map/pallas_call | solution.py:231
  83.2 14.2 %all_to_all.16.pieces_ref = bf16[8,4,64,128]{3,2,1,0:T(8,128)(2,1)} all-to-all(bf16[8,4,64,128]{3,2,1,0:T(8,128)(2,1)S(1)} %bitcast.10), channel_id=1, replica_groups=mesh['sub'=8,'beam'=16] {'sub'}, dimensions={0} | all-to-all | bytes 1048576 | tf_op jit(solution)/shard_map/all_to_all | solution.py:285
  97.4 1.9 %shard_map.72 = f32[4,64,128]{2,1,0:T(8,128)} custom-call(bf16[8,4,64,128]{3,2,1,0:T(8,128)(2,1)} %all_to_all.16.pieces_ref), custom_call_target="tpu_custom_call" | custom-call | tf_op jit(solution)/shard_map/pallas_call | solution.py:265
Async XLA Ops:
  0.6 1.0 %copy-start = (bf16[4,128,512]{2,1,0:T(8,128)(2,1)S(1)}, bf16[4,128,512]{2,1,0:T(8,128)(2,1)}, u32[]{:S(2)}) copy-start(bf16[4,128,512]{2,1,0:T(8,128)(2,1)} %constant.2.clone.table_ref) | copy-start | bytes 1572868
  1.7 20.9 %copy-start.2 = (s32[1024]{0:T(1024)S(1)}, s32[1024]{0:T(1024)}, u32[]{:S(2)}) copy-start(s32[1024]{0:T(1024)} %param.7) | copy-start | bytes 12292
  11.4 41.5 %all-to-all-start = ((bf16[128,4,8,256]{3,2,1,0:T(8,128)(2,1)}), bf16[128,4,8,256]{3,2,1,0:T(8,128)(2,1)S(1)}, u32[]{:S(2)}, u32[]{:S(2)}) async-start(bf16[128,4,8,256]{3,2,1,0:T(8,128)(2,1)} %bitcast.13), calls=%async_computation | async-start | bytes 4194304 | tf_op jit(solution)/shard_map/all_to_all | solution.py:278
  36.6 42.5 %copy-start.1 = (s32[32,32]{1,0:T(8,128)S(1)}, s32[32,32]{1,0:T(8,128)}, u32[]{:S(2)}) copy-start(s32[32,32]{1,0:T(8,128)} %delay_ref.1) | copy-start | bytes 12292

commit v3 on v2

--- a/solution.py
+++ b/solution.py
@@ -6,7 +6,7 @@
 from jax import lax
 from jax.experimental import pallas as pl
 from jax.experimental.pallas import tpu as pltpu
-from jax.sharding import PartitionSpec as P
+from jax.sharding import Mesh, PartitionSpec as P
 
 A = 1024
 NFFT = 1024
@@ -15,6 +15,11 @@
 OUT = 128
 FR = 256
 HALF = OUT // 2
+AXES = (("zh", 2), ("x", 4), ("zl", 2), ("y", 4), ("core", 2))
+EVERY = tuple(name for name, size in AXES)
+SIZES = tuple(size for name, size in AXES)
+ORDER = ("core", "x", "y", "zh", "zl")
+TURN = tuple(EVERY.index(name) for name in ORDER)
 ROWS = FR - HALF
 
 
@@ -31,6 +36,7 @@
     return rows.reshape(4, C // 2, NFFT // 2).astype(jnp.bfloat16)
 
 
+PLACE = np.argsort(np.arange(C // 2).reshape(SIZES).transpose(TURN).reshape(-1)).tolist()
 PITCH = 20
 SPAN = 65
 FRAMES = 16
@@ -103,8 +109,10 @@
         for side in range(2):
             lanes = slice(side * 128, side * 128 + 128)
             for q in range(C // 4):
-                block = done_ref[side, SPAN * q : SPAN * q + 64, :]
-                out_ref[8 * q : 8 * q + 8, :, lanes] = block.reshape(8, 8, 128).astype(jnp.bfloat16)
+                block = done_ref[side, SPAN * q : SPAN * q + 64, :].reshape(8, 8, 128).astype(jnp.bfloat16)
+                for core in range(2):
+                    start = 4 * PLACE[2 * q + core]
+                    out_ref[start : start + 4, :, lanes] = block[4 * core : 4 * core + 4]
 
 
 def channelize(voltages):
@@ -112,7 +120,7 @@
     rows = FR * 16
     flat = voltages.reshape(antennas, FR, 2, 8, 128).transpose(0, 1, 3, 2, 4).reshape(antennas * rows, 128)
     flat = pltpu.with_memory_space_constraint(flat, pltpu.HBM)
-    table = jnp.asarray(dft_table())
+    table = pltpu.with_memory_space_constraint(jnp.asarray(dft_table()), pltpu.HBM)
     mixed = pltpu.VMEM((4, FR, NFFT // 2), jnp.bfloat16)
     wide = pltpu.VMEM((FR * PITCH, 128), jnp.float32)
     return pl.pallas_call(
@@ -191,28 +199,36 @@
     )(spectra, pltpu.with_memory_space_constraint(weights, pltpu.HBM))
 
 
-def dedisperse_kernel(delay_ref, power_ref, out_ref, kept_ref, turned_ref, sem):
-    channels, beams = power_ref.shape[:2]
-    keep = pltpu.make_async_copy(power_ref, kept_ref, sem)
-    keep.start()
+def dedisperse_kernel(delay_ref, core_ref, near_ref, far_ref, out_ref, kept_ref, turned_ref, sems):
+    chips, _, owned, beams = near_ref.shape[:4]
+    channels = chips * 2 * owned
+    core = core_ref[0]
+    copies = [
+        pltpu.make_async_copy(near_ref.at[:, core], kept_ref.at[:, core], sems.at[0]),
+        pltpu.make_async_copy(far_ref, kept_ref.at[:, 1 - core], sems.at[1]),
+    ]
+    for copy in copies:
+        copy.start()
     rows = lax.broadcasted_iota(jnp.int32, (ROWS, FR), 0)
     lanes = lax.broadcasted_iota(jnp.int32, (ROWS, FR), 1)
     unit = jnp.where(rows == lanes, 1.0, 0.0).astype(jnp.bfloat16)
 
-    for pair in range(channels // 2):
-        parts = []
-        for c in range(2):
-            power = power_ref[2 * pair + c]
-            parts += [power, jnp.concatenate([power[:, HALF:], power[:, :HALF]], axis=1)]
-        both = lax.dot_general(
-            unit,
-            jnp.concatenate(parts, axis=0),
-            (((1,), (1,)), ((), ())),
-            preferred_element_type=jnp.float32,
-        )
-        for c in range(2):
-            start = (2 * pair + c) * ROWS
-            turned_ref[start : start + ROWS, :] = both[:, c * 2 * beams : (c + 1) * 2 * beams]
+    for chip in range(chips):
+        for side in range(2):
+            parts = []
+            for k in range(owned):
+                power = near_ref[chip, core, k] if side == 0 else far_ref[chip, k]
+                parts += [power, jnp.concatenate([power[:, HALF:], power[:, :HALF]], axis=1)]
+            both = lax.dot_general(
+                unit,
+                jnp.concatenate(parts, axis=0),
+                (((1,), (1,)), ((), ())),
+                preferred_element_type=jnp.float32,
+            )
+            source = core if side == 0 else 1 - core
+            for k in range(owned):
+                start = pl.multiple_of(((chip * 2 + source) * owned + k) * ROWS, 8)
+                turned_ref[pl.ds(start, ROWS), :] = both[:, k * 2 * beams : (k + 1) * 2 * beams]
 
     def trial(pair, carry):
         for t in (2 * pair, 2 * pair + 1):
@@ -223,15 +239,19 @@
         return carry
 
     lax.fori_loop(0, TRIALS // 2, trial, 0)
-    keep.wait()
-
-
-def dedisperse(filterbank, delays):
-    channels, beams = filterbank.shape[:2]
+    for copy in copies:
+        copy.wait()
+
+
+def dedisperse(delays, core, near, far):
+    chips, _, owned, beams = near.shape[:4]
+    channels = chips * 2 * owned
     return pl.pallas_call(
         dedisperse_kernel,
         in_specs=[
             pl.BlockSpec(memory_space=pltpu.SMEM),
+            pl.BlockSpec(memory_space=pltpu.SMEM),
+            pl.BlockSpec(memory_space=pltpu.VMEM),
             pl.BlockSpec(memory_space=pltpu.VMEM),
         ],
         out_specs=(
@@ -240,14 +260,14 @@
         ),
         out_shape=(
             jax.ShapeDtypeStruct((TRIALS, HALF, 2 * beams), jnp.bfloat16),
-            jax.ShapeDtypeStruct(filterbank.shape, filterbank.dtype),
+            jax.ShapeDtypeStruct(near.shape, near.dtype),
         ),
         scratch_shapes=[
             pltpu.VMEM((channels * ROWS, 2 * beams), jnp.float32),
-            pltpu.SemaphoreType.DMA,
+            pltpu.SemaphoreType.DMA((2,)),
         ],
         compiler_params=pltpu.CompilerParams(vmem_limit_bytes=16 << 20),
-    )(delays, filterbank)
+    )(delays, core.reshape(1), near, far)
 
 
 def sum_kernel(pieces_ref, out_ref):
@@ -269,34 +289,40 @@
 
 
 def on_device(voltages, weights, antenna_map, delays):
-    subband_count = lax.axis_size("sub")
-    beam_count = lax.axis_size("beam")
-    devices = subband_count * beam_count
-    owned = C // devices
+    sub, beam = EVERY[:2], EVERY[2:]
+    subband_count, beam_count = lax.axis_size(sub), lax.axis_size(beam)
+    owned = weights.shape[0]
+    core = lax.axis_index("core")
     spectra = channelize(voltages)
-    spectra = spectra.reshape(devices, owned * 2, voltages.shape[0], FR)
-    moved = lax.all_to_all(spectra, ("sub", "beam"), 0, 0, tiled=True)
-    ordered = order_weights(antenna_map, weights)
+    spectra = spectra.reshape(-1, owned * 2, voltages.shape[0], FR)
+    moved = lax.all_to_all(spectra, ORDER, 0, 0, tiled=True)
+    arrived = antenna_map.reshape(*SIZES, -1).transpose(*TURN, len(SIZES)).reshape(A)
+    ordered = order_weights(arrived, weights)
     power = form_beams(moved, ordered, beam_count)
-    filterbank = lax.all_to_all(power, "beam", 0, 0, tiled=True)
+    power = power.reshape(beam_count // 2, 2, *power.shape[1:])
+    near = lax.all_to_all(power, ("zl", "y"), 0, 0, tiled=True)
+    away = lax.dynamic_index_in_dim(near, 1 - core, 1, keepdims=False)
+    far = lax.ppermute(away, "core", [(0, 1), (1, 0)])
+    partial, filterbank = dedisperse(delays, core, near, far)
     filterbank = filterbank.reshape(beam_count * owned, -1, FR)
-    partial, filterbank = dedisperse(filterbank, delays)
     pieces = partial.reshape(subband_count, TRIALS // subband_count, *partial.shape[1:])
-    series = sum_pieces(lax.all_to_all(pieces, "sub", 0, 0, tiled=True))
+    series = sum_pieces(lax.all_to_all(pieces, sub, 0, 0, tiled=True))
     return (filterbank, series)
 
 
 def solution(mesh):
+    sub, beam = EVERY[:2], EVERY[2:]
+    fine = Mesh(mesh.devices.reshape(SIZES), EVERY)
     placed = (
-        P(("sub", "beam"), None, None, None),
-        P(("sub", "beam"), None, None, None),
+        P(EVERY, None, None, None),
+        P(EVERY, None, None, None),
         P(),
-        P("sub", None),
+        P(sub, None),
     )
     return jax.shard_map(
         on_device,
-        mesh=mesh,
+        mesh=fine,
         in_specs=placed,
-        out_specs=(P("sub", "beam", None), P("sub", "beam", None)),
+        out_specs=(P(sub, beam, None), P(sub, beam, None)),
         check_vma=False,
     )

time: 100 us -> 103 us (1.030)
  blocking collectives: 33.3 us -> 16.7 us
  waiting for transfers between devices: 16.3 us -> 30.9 us
  starting transfers between devices: 11.2 us -> 15.9 us
    all_to_all x2 -> x1, blocking collectives: 33.3 us -> 16.7 us  [on_device(): series = sum_pieces(lax.all_to_all(pieces, sub, 0, 0, tiled=True))]
    all_to_all x1 -> x2, waiting for transfers between devices: 16.3 us -> 29 us  [the longest x1 15.3 us: on_device(): near = lax.all_to_all(power, ('zl', 'y'), 0, 0, tiled=True)]
    all_to_all x1 -> x2, starting transfers between devices: 11.2 us -> 15.8 us  [the longest x1 11.2 us: on_device(): moved = lax.all_to_all(spectra, ORDER, 0, 0, tiled=True)]
    ppermute x0 -> x1, waiting for transfers between devices: none -> 1.9 us  [on_device(): far = lax.ppermute(away, 'core', [(0, 1), (1, 0)])]
    unnamed x6 -> x4, local copies, waits for them, and re-layouts: 1.04 us -> 0.01 us
  transfers between devices with their start and end apart: 1 -> 3, of which waited for: 1 -> 3; matrix products, arithmetic and copies ran while one was open for 0% -> 0% of each run, Pallas kernels for 14% -> 14%
where the time goes in v3:
time: 103 us; the launch traced here: 102 us
  Pallas kernels  37.7 us (37%)
  waiting for transfers between devices  30.9 us (30%)
  blocking collectives  16.7 us (16%)
  starting transfers between devices  15.9 us (15%)
    all_to_all x1, blocking collectives, on_device(): series = sum_pieces(lax.all_to_all(pieces, sub, 0, 0, tiled=True))  16.7 us
    all_to_all x1, waiting for transfers between devices, on_device(): near = lax.all_to_all(power, ('zl', 'y'), 0, 0, tiled=True)  15.3 us
    pallas_call x1, Pallas kernels, order_weights(): pl.pallas_call(order_kernel, grid=(owned, beams // block), in_specs=[pl.B...  14 us
    all_to_all x1, waiting for transfers between devices, on_device(): moved = lax.all_to_all(spectra, ORDER, 0, 0, tiled=True)  13.7 us
    all_to_all x1, starting transfers between devices, on_device(): moved = lax.all_to_all(spectra, ORDER, 0, 0, tiled=True)  11.2 us
    pallas_call x1, Pallas kernels, channelize(): pl.pallas_call(channel_kernel, grid=(antennas // PAIR,), in_specs=[pl.Blo...  9.79 us
    pallas_call x1, Pallas kernels, form_beams(): pl.pallas_call(beam_kernel, grid=(owned, beams // block), in_specs=[pl.Bl...  7.83 us
    all_to_all x1, starting transfers between devices, on_device(): near = lax.all_to_all(power, ('zl', 'y'), 0, 0, tiled=True)  4.67 us
  transfers between devices with their start and end apart: 3, of which 3 were waited for; matrix products, arithmetic and copies ran while one was open for 0% of the time, Pallas kernels for 14%

profile of v3, /device:TPU:0, one launch (start us, length us, event | category | flops | bytes accessed | tf_op | source)
XLA Modules:
  0.0 102.3 jit_solution(1036444755118421854)
XLA Ops:
  0.6 0.0 copy-start.1
  0.6 9.8 %shard_map.68 = bf16[512,8,256]{2,1,0:T(8,128)(2,1)} custom-call(bf16[4,128,512]{2,1,0:T(8,128)(2,1)} %constant.15.clone.table_ref, bf16[32768,128]{1,0:T(8,128)(2,1)} %bitcast.14), custom_call_target="tpu_custom_call" | custom-call | tf_op jit(solution)/shard_map/pallas_call | solution.py:126
  10.4 11.2 %all-to-all-start = ((bf16[128,4,8,256]{3,2,1,0:T(8,128)(2,1)}), bf16[128,4,8,256]{3,2,1,0:T(8,128)(2,1)S(1)}, u32[]{:S(2)}, u32[]{:S(2)}) async-start(bf16[128,4,8,256]{3,2,1,0:T(8,128)(2,1)} %bitcast.15), calls=%async_computation | async-start | bytes 4194304 | tf_op jit(solution)/shard_map/all_to_all | solution.py:298
  21.6 0.0 copy-done.1
  21.6 0.1 reshape.32
  21.8 0.1 reshape_reshape.3.map_ref
  21.9 14.0 %shard_map.69.weight_ref = bf16[2,2,1024,1024]{3,2,1,0:T(8,128)(2,1)} custom-call(s32[1,1024]{1,0:T(1,128)S(1)} %reshape_reshape.3.map_ref, bf16[2,2,1024,1024]{3,2,1,0:T(8,128)(2,1)} %weight_ref.1), custom_call_target="tpu_custom_call" | custom-call | tf_op jit(solution)/shard_map/pallas_call | solution.py:172
  35.9 0.0 copy-start
  35.9 13.7 %all-to-all-done.spectra_ref = bf16[128,4,8,256]{3,2,1,0:T(8,128)(2,1)S(1)} async-done(((bf16[128,4,8,256]{3,2,1,0:T(8,128)(2,1)}), bf16[128,4,8,256]{3,2,1,0:T(8,128)(2,1)S(1)}, u32[]{:S(2)}, u32[]{:S(2)}) %all-to-all-start) | async-done | bytes 2097184 | tf_op jit(solution)/shard_map/all_to_all | solution.py:298
  49.7 7.8 %shard_map.70 = bf16[16,2,64,256]{3,2,1,0:T(8,128)(2,1)} custom-call(bf16[128,4,8,256]{3,2,1,0:T(8,128)(2,1)S(1)} %all-to-all-done.spectra_ref, bf16[2,2,1024,1024]{3,2,1,0:T(8,128)(2,1)} %shard_map.69.weight_ref), custom_call_target="tpu_custom_call" | custom-call | tf_op jit(solution)/shard_map/pallas_call | solution.py:188
  57.5 4.7 %all-to-all-start.1 = ((bf16[8,2,2,64,256]{4,3,2,1,0:T(8,128)(2,1)}), bf16[8,2,2,64,256]{4,3,2,1,0:T(8,128)(2,1)S(1)}, u32[]{:S(2)}, u32[]{:S(2)}) async-start(bf16[8,2,2,64,256]{4,3,2,1,0:T(8,128)(2,1)} %bitcast.6), calls=%async_computation.1 | async-start | bytes 2097152 | tf_op jit(solution)/shard_map/all_to_all | solution.py:303
  62.2 15.3 %all-to-all-done.1.near_ref = bf16[8,2,2,64,256]{4,3,2,1,0:T(8,128)(2,1)S(1)} async-done(((bf16[8,2,2,64,256]{4,3,2,1,0:T(8,128)(2,1)}), bf16[8,2,2,64,256]{4,3,2,1,0:T(8,128)(2,1)S(1)}, u32[]{:S(2)}, u32[]{:S(2)}) %all-to-all-start.1) | async-done | bytes 1048608 | tf_op jit(solution)/shard_map/all_to_all | solution.py:303
  77.5 0.1 collective-permute-start
  77.6 1.9 %collective-permute-done.far_ref = bf16[8,2,64,256]{3,2,1,0:T(8,128)(2,1)S(1)} collective-permute-done((bf16[8,2,64,256]{3,2,1,0:T(8,128)(2,1)S(1)}, bf16[8,2,64,256]{3,2,1,0:T(8,128)(2,1)S(1)}, u32[]{:S(2)}, u32[]{:S(2)}) %collective-permute-start) | collective-permute-done | bytes 524320 | tf_op jit(solution)/shard_map/ppermute | solution.py:305
  79.5 0.0 copy-done
  79.5 4.2 %shard_map.71 = (bf16[32,64,128]{2,1,0:T(8,128)(2,1)S(1)}, bf16[8,2,2,64,256]{4,3,2,1,0:T(8,128)(2,1)}) custom-call(s32[32,32]{1,0:T(8,128)S(1)} %copy-done, s32[1]{0:T(128)} %bitcast.core_ref, bf16[8,2,2,64,256]{4,3,2,1,0:T(8,128)(2,1)S(1)} %all-to-all-done.1.near_ref, bf16[8,2,64,256]{3,2,1,0:T(8,128)(2,1)S(1)} %collective-permute-done.far_ref), custom_call_target="tpu_custom_call" | custom-call | tf_op jit(solution)/shard_map/pallas_call | solution.py:249
  83.7 16.7 %all_to_all.15.pieces_ref = bf16[8,4,64,128]{3,2,1,0:T(8,128)(2,1)} all-to-all(bf16[8,4,64,128]{3,2,1,0:T(8,128)(2,1)S(1)} %bitcast.13), channel_id=1, replica_groups=mesh['zh'=2,'x'=4,'zl'=2,'y'=4,'core'=2] {'zh','x'}, dimensions={0} | all-to-all | bytes 1048576 | tf_op jit(solution)/shard_map/all_to_all | solution.py:309
  100.4 1.9 %shard_map.72 = f32[4,64,128]{2,1,0:T(8,128)} custom-call(bf16[8,4,64,128]{3,2,1,0:T(8,128)(2,1)} %all_to_all.15.pieces_ref), custom_call_target="tpu_custom_call" | custom-call | tf_op jit(solution)/shard_map/pallas_call | solution.py:285
  (2 shorter events, 0.1 us)
Async XLA Ops:
  0.6 21.0 %copy-start.1 = (s32[1024]{0:T(1024)S(1)}, s32[1024]{0:T(1024)}, u32[]{:S(2)}) copy-start(s32[1024]{0:T(1024)} %param.7) | copy-start | bytes 12292
  10.4 39.3 %all-to-all-start = ((bf16[128,4,8,256]{3,2,1,0:T(8,128)(2,1)}), bf16[128,4,8,256]{3,2,1,0:T(8,128)(2,1)S(1)}, u32[]{:S(2)}, u32[]{:S(2)}) async-start(bf16[128,4,8,256]{3,2,1,0:T(8,128)(2,1)} %bitcast.15), calls=%async_computation | async-start | bytes 4194304 | tf_op jit(solution)/shard_map/all_to_all | solution.py:298
  35.9 43.5 %copy-start = (s32[32,32]{1,0:T(8,128)S(1)}, s32[32,32]{1,0:T(8,128)}, u32[]{:S(2)}) copy-start(s32[32,32]{1,0:T(8,128)} %delay_ref.1) | copy-start | bytes 12292
  57.5 19.9 %all-to-all-start.1 = ((bf16[8,2,2,64,256]{4,3,2,1,0:T(8,128)(2,1)}), bf16[8,2,2,64,256]{4,3,2,1,0:T(8,128)(2,1)S(1)}, u32[]{:S(2)}, u32[]{:S(2)}) async-start(bf16[8,2,2,64,256]{4,3,2,1,0:T(8,128)(2,1)} %bitcast.6), calls=%async_computation.1 | async-start | bytes 2097152 | tf_op jit(solution)/shard_map/all_to_all | solution.py:303
  77.5 2.0 %collective-permute-start = (bf16[8,2,64,256]{3,2,1,0:T(8,128)(2,1)S(1)}, bf16[8,2,64,256]{3,2,1,0:T(8,128)(2,1)S(1)}, u32[]{:S(2)}, u32[]{:S(2)}) collective-permute-start(bf16[8,2,64,256]{3,2,1,0:T(8,128)(2,1)S(1)} %dynamic-slice_bitcast_fusion), channel_id=1, source_target_pairs={{0,1},{1,0},{2,3},{3,2},{4,5},{5,4},{6,7},{7,6},{8,9},{9,8},{10,11... | collective-permute-start | bytes 1572872 | tf_op jit(solution)/shard_map/ppermute | solution.py:305

commit v4 on v2

--- a/solution.py
+++ b/solution.py
@@ -6,7 +6,7 @@
 from jax import lax
 from jax.experimental import pallas as pl
 from jax.experimental.pallas import tpu as pltpu
-from jax.sharding import PartitionSpec as P
+from jax.sharding import Mesh, PartitionSpec as P
 
 A = 1024
 NFFT = 1024
@@ -15,6 +15,12 @@
 OUT = 128
 FR = 256
 HALF = OUT // 2
+AXES = (("zh", 2), ("x", 4), ("zl", 2), ("y", 4), ("core", 2))
+EVERY = tuple(name for name, size in AXES)
+SIZES = tuple(size for name, size in AXES)
+ORDER = ("core", "x", "y", "zh", "zl")
+TURN = tuple(EVERY.index(name) for name in ORDER)
+CHIPS = np.arange(C // 4).reshape(SIZES[:-1]).transpose(TURN[1:]).reshape(-1).tolist()
 ROWS = FR - HALF
 
 
@@ -31,57 +37,53 @@
     return rows.reshape(4, C // 2, NFFT // 2).astype(jnp.bfloat16)
 
 
-PITCH = 20
 SPAN = 65
-FRAMES = 16
+BLOCK = 1024
+SUBBLOCK = 512
 PAIR = 2
 
 
-def mix_frames(sample_ref, wide_ref, mixed_ref, row, first):
-    for f in range(FRAMES):
-        start = row + (first + f) * 16
-        wide_ref[PITCH * (first + f) : PITCH * (first + f) + 16, :] = sample_ref[start : start + 16, :].astype(jnp.float32)
-
-    def pick(block, part):
-        return wide_ref[pl.ds(PITCH * first + 2 * block + part, FRAMES, stride=PITCH), :]
-
-    for half in range(2):
-        re = [pick(2 * j + half, 0) for j in range(4)]
-        im = [pick(2 * j + half, 1) for j in range(4)]
-        add_re, sub_re = re[0] + re[2], re[0] - re[2]
-        add_im, sub_im = im[0] + im[2], im[0] - im[2]
-        odd_add_re, odd_sub_re = re[1] + re[3], re[1] - re[3]
-        odd_add_im, odd_sub_im = im[1] + im[3], im[1] - im[3]
-        mixed = (
-            (add_re + odd_add_re, add_im + odd_add_im),
-            (sub_re + odd_sub_im, sub_im - odd_sub_re),
-            (add_re - odd_add_re, add_im - odd_add_im),
-            (sub_re - odd_sub_im, sub_im + odd_sub_re),
-        )
-        for r in range(4):
-            for part in range(2):
-                lane = part * 256 + half * 128
-                mixed_ref[r, first : first + FRAMES, lane : lane + 128] = mixed[r][part].astype(jnp.bfloat16)
-
-
-def transform(table_ref, mixed_ref, done_ref, antenna):
+def mix_table():
+    turn = np.array([1, -1j, -1, 1j])
+    table = np.zeros((4, 2, 2, 16, 16, 4, 2, 2))
+    for r in range(4):
+        for j in range(4):
+            c = turn[r * j % 4]
+            for half in range(2):
+                for f in range(16):
+                    table[r, 0, half, f, f, j, half] = (c.real, -c.imag)
+                    table[r, 1, half, f, f, j, half] = (c.imag, c.real)
+    return table.reshape(256, 256).astype(jnp.bfloat16)
+
+
+def mix_frames(mix_ref, sample_ref, mixed_ref, row, p):
+    start = row + p * 512
+    block = jnp.concatenate([sample_ref[start : start + 256, :], sample_ref[start + 256 : start + 512, :]], axis=1)
+    got = jnp.dot(mix_ref[...], block, preferred_element_type=jnp.float32).astype(jnp.bfloat16)
+    for k in range(16):
+        r, lane = k // 4, k % 4 * 128
+        for side in range(2):
+            first = p * 32 + side * 16
+            mixed_ref[r, first : first + 16, lane : lane + 128] = got[16 * k : 16 * k + 16, side * 128 : side * 128 + 128]
+
+
+def transform(table_ref, mixed_ref, done_ref, antenna, r):
     groups = C // 4
-    for r in range(4):
-        got = lax.dot_general(
-            table_ref[r],
-            mixed_ref[r],
-            (((1,), (1,)), ((), ())),
-            preferred_element_type=jnp.float32,
-        )
-        for part in range(2):
-            start = r * 16 + part * 8 + antenna
-            for side in range(2):
-                done_ref[side, pl.ds(start, groups, stride=SPAN), :] = got[
-                    part * groups : part * groups + groups, side * 128 : side * 128 + 128
-                ]
-
-
-def channel_kernel(table_ref, sample_ref, out_ref, wide_a, wide_b, mixed_a, mixed_b, done_ref):
+    got = lax.dot_general(
+        table_ref[r],
+        mixed_ref[r],
+        (((1,), (1,)), ((), ())),
+        preferred_element_type=jnp.float32,
+    )
+    for part in range(2):
+        start = r * 16 + part * 8 + antenna
+        for side in range(2):
+            done_ref[side, pl.ds(start, groups, stride=SPAN), :] = got[
+                part * groups : part * groups + groups, side * 128 : side * 128 + 128
+            ]
+
+
+def channel_kernel(table_ref, mix_ref, sample_ref, out_ref, mixed_a, mixed_b, done_ref, stage_ref, sems):
     antenna = pl.program_id(0) * PAIR
     last = PAIR * (pl.num_programs(0) - 1)
     before = jnp.where(antenna == 0, last + 1, antenna - 1)
@@ -90,21 +92,36 @@
     def _():
         mixed_b[...] = jnp.zeros(mixed_b.shape, mixed_b.dtype)
 
-    transform(table_ref, mixed_b, done_ref, before)
-    for first in range(0, FR, FRAMES):
-        mix_frames(sample_ref, wide_a, mixed_a, 0, first)
-    transform(table_ref, mixed_a, done_ref, antenna)
-    for first in range(0, FR, FRAMES):
-        mix_frames(sample_ref, wide_b, mixed_b, FR * 16, first)
+    for p in range(8):
+        mix_frames(mix_ref, sample_ref, mixed_a, 0, p)
+        if p % 2 == 0:
+            transform(table_ref, mixed_b, done_ref, before, p // 2)
+    for p in range(8):
+        mix_frames(mix_ref, sample_ref, mixed_b, FR * 16, p)
+        if p % 2 == 0:
+            transform(table_ref, mixed_a, done_ref, antenna, p // 2)
 
     @pl.when(antenna == last)
     def _():
-        transform(table_ref, mixed_b, done_ref, antenna + 1)
-        for side in range(2):
-            lanes = slice(side * 128, side * 128 + 128)
-            for q in range(C // 4):
-                block = done_ref[side, SPAN * q : SPAN * q + 64, :]
-                out_ref[8 * q : 8 * q + 8, :, lanes] = block.reshape(8, 8, 128).astype(jnp.bfloat16)
+        for r in range(4):
+            transform(table_ref, mixed_b, done_ref, antenna + 1, r)
+        sends = []
+        half = C
+        for place, q in enumerate(CHIPS):
+            for side in range(2):
+                lanes = slice(side * 128, side * 128 + 128)
+                block = done_ref[side, SPAN * q : SPAN * q + 64, :].reshape(8, 8, 128).astype(jnp.bfloat16)
+                for core in range(2):
+                    start = core * half + 4 * place
+                    stage_ref[start : start + 4, :, lanes] = block[4 * core : 4 * core + 4]
+            if place % 16 == 15:
+                for core in range(2):
+                    rows = pl.ds(core * half + 4 * (place - 15), 64)
+                    sem = sems.at[core, place // 16]
+                    sends.append(pltpu.make_async_copy(stage_ref.at[rows], out_ref.at[rows], sem))
+                    sends[-1].start()
+        for send in sends:
+            send.wait()
 
 
 def channelize(voltages):
@@ -112,30 +129,39 @@
     rows = FR * 16
     flat = voltages.reshape(antennas, FR, 2, 8, 128).transpose(0, 1, 3, 2, 4).reshape(antennas * rows, 128)
     flat = pltpu.with_memory_space_constraint(flat, pltpu.HBM)
-    table = jnp.asarray(dft_table())
+    table = pltpu.with_memory_space_constraint(jnp.asarray(dft_table()), pltpu.HBM)
+    mix = pltpu.with_memory_space_constraint(jnp.asarray(mix_table()), pltpu.HBM)
     mixed = pltpu.VMEM((4, FR, NFFT // 2), jnp.bfloat16)
-    wide = pltpu.VMEM((FR * PITCH, 128), jnp.float32)
     return pl.pallas_call(
         channel_kernel,
         grid=(antennas // PAIR,),
         in_specs=[
             pl.BlockSpec(table.shape, lambda a: (0, 0, 0)),
+            pl.BlockSpec(mix.shape, lambda a: (0, 0)),
             pl.BlockSpec((PAIR * rows, 128), lambda a: (a, 0)),
         ],
-        out_specs=pl.BlockSpec((2 * C, antennas, FR), lambda a: (0, 0, 0)),
+        out_specs=pl.BlockSpec(memory_space=pltpu.HBM),
         out_shape=pltpu.HBM((2 * C, antennas, FR), jnp.bfloat16),
-        scratch_shapes=[wide, wide, mixed, mixed, pltpu.VMEM((2, C // 4 * SPAN, 128), jnp.float32)],
+        scratch_shapes=[
+            mixed,
+            mixed,
+            pltpu.VMEM((2, C // 4 * SPAN, 128), jnp.float32),
+            pltpu.VMEM((2 * C, antennas, FR), jnp.bfloat16),
+            pltpu.SemaphoreType.DMA((2, 4)),
+        ],
         compiler_params=pltpu.CompilerParams(vmem_limit_bytes=32 << 20),
-    )(table, flat)
+    )(table, mix, flat)
 
 
 def beam_kernel(spectra_ref, weight_ref, power_ref, data_ref):
+    channel = pl.program_id(0)
+
     @pl.when(pl.program_id(1) == 0)
     def _():
         for part in range(2):
-            data_ref[:, part * FR : (part + 1) * FR] = spectra_ref[:, part].reshape(A, FR)
-
-    block = 256
+            data_ref[:, part * FR : (part + 1) * FR] = spectra_ref[:, 2 * channel + part].reshape(A, FR)
+
+    block = SUBBLOCK
     width = power_ref.shape[2]
     for first in range(0, weight_ref.shape[2], block):
         both = weight_ref[0, :, first : first + block].reshape(2 * block, A)
@@ -143,7 +169,8 @@
         beam_re = made[:block, :FR] - made[block:, FR:]
         beam_im = made[:block, FR:] + made[block:, :FR]
         power = (beam_re * beam_re + beam_im * beam_im).astype(jnp.bfloat16)
-        power_ref[first // width : (first + block) // width, 0] = power.reshape(block // width, width, FR)
+        place = (pl.program_id(1) * weight_ref.shape[2] + first) // width
+        power_ref[pl.ds(place, block // width), channel] = power.reshape(block // width, width, FR)
 
 
 def order_kernel(map_ref, weight_ref, out_ref, place_ref):
@@ -174,17 +201,16 @@
 
 def form_beams(spectra, weights, beam_count):
     owned, beams = weights.shape[0], weights.shape[2]
-    block = 1024
+    block = BLOCK
     width = beams // beam_count
-    per_block = block // width
     return pl.pallas_call(
         beam_kernel,
         grid=(owned, beams // block),
         in_specs=[
-            pl.BlockSpec((spectra.shape[0], 2, spectra.shape[2], FR), lambda k, b: (0, k, 0, 0)),
+            pl.BlockSpec(memory_space=pltpu.VMEM),
             pl.BlockSpec((1, 2, block, A), lambda k, b: (k, 0, b, 0)),
         ],
-        out_specs=pl.BlockSpec((per_block, 1, width, FR), lambda k, b: (b, k, 0, 0)),
+        out_specs=pl.BlockSpec(memory_space=pltpu.VMEM),
         out_shape=jax.ShapeDtypeStruct((beam_count, owned, width, FR), jnp.bfloat16),
         scratch_shapes=[pltpu.VMEM((A, 2 * FR), jnp.bfloat16)],
         compiler_params=pltpu.CompilerParams(vmem_limit_bytes=32 << 20),
@@ -269,34 +295,36 @@
 
 
 def on_device(voltages, weights, antenna_map, delays):
-    subband_count = lax.axis_size("sub")
-    beam_count = lax.axis_size("beam")
-    devices = subband_count * beam_count
-    owned = C // devices
+    sub, beam = EVERY[:2], EVERY[2:]
+    subband_count, beam_count = lax.axis_size(sub), lax.axis_size(beam)
+    owned = weights.shape[0]
     spectra = channelize(voltages)
-    spectra = spectra.reshape(devices, owned * 2, voltages.shape[0], FR)
-    moved = lax.all_to_all(spectra, ("sub", "beam"), 0, 0, tiled=True)
-    ordered = order_weights(antenna_map, weights)
+    spectra = spectra.reshape(-1, owned * 2, voltages.shape[0], FR)
+    moved = lax.all_to_all(spectra, ORDER, 0, 0, tiled=True)
+    arrived = antenna_map.reshape(*SIZES, -1).transpose(*TURN, len(SIZES)).reshape(A)
+    ordered = order_weights(arrived, weights)
     power = form_beams(moved, ordered, beam_count)
-    filterbank = lax.all_to_all(power, "beam", 0, 0, tiled=True)
+    filterbank = lax.all_to_all(power, beam, 0, 0, tiled=True)
     filterbank = filterbank.reshape(beam_count * owned, -1, FR)
     partial, filterbank = dedisperse(filterbank, delays)
     pieces = partial.reshape(subband_count, TRIALS // subband_count, *partial.shape[1:])
-    series = sum_pieces(lax.all_to_all(pieces, "sub", 0, 0, tiled=True))
+    series = sum_pieces(lax.all_to_all(pieces, sub, 0, 0, tiled=True))
     return (filterbank, series)
 
 
 def solution(mesh):
+    sub, beam = EVERY[:2], EVERY[2:]
+    fine = Mesh(mesh.devices.reshape(SIZES), EVERY)
     placed = (
-        P(("sub", "beam"), None, None, None),
-        P(("sub", "beam"), None, None, None),
+        P(EVERY, None, None, None),
+        P(EVERY, None, None, None),
         P(),
-        P("sub", None),
+        P(sub, None),
     )
     return jax.shard_map(
         on_device,
-        mesh=mesh,
+        mesh=fine,
         in_specs=placed,
-        out_specs=(P("sub", "beam", None), P("sub", "beam", None)),
+        out_specs=(P(sub, beam, None), P(sub, beam, None)),
         check_vma=False,
     )

time: 100 us -> 98.9 us (0.989)
  blocking collectives: 33.3 us -> 35.9 us
  waiting for transfers between devices: 16.3 us -> 13.8 us
    all_to_all x2, blocking collectives: 33.3 us -> 35.9 us  [the longest x1 21 us: on_device(): filterbank = lax.all_to_all(power, beam, 0, 0, tiled=True)]
    all_to_all x1, waiting for transfers between devices: 16.3 us -> 13.8 us  [on_device(): moved = lax.all_to_all(spectra, ORDER, 0, 0, tiled=True)]
    unnamed x6 -> x4, local copies, waits for them, and re-layouts: 1.04 us -> 0.01 us
where the time goes in v4:
time: 98.9 us; the launch traced here: 98.3 us
  Pallas kernels  36.4 us (37%)
  blocking collectives  35.9 us (36%)
  waiting for transfers between devices  13.8 us (14%)
  starting transfers between devices  11.2 us (11%)
    all_to_all x1, blocking collectives, on_device(): filterbank = lax.all_to_all(power, beam, 0, 0, tiled=True)  21 us
    all_to_all x1, blocking collectives, on_device(): series = sum_pieces(lax.all_to_all(pieces, sub, 0, 0, tiled=True))  14.9 us
    pallas_call x1, Pallas kernels, order_weights(): pl.pallas_call(order_kernel, grid=(owned, beams // block), in_specs=[pl.B...  14 us
    all_to_all x1, waiting for transfers between devices, on_device(): moved = lax.all_to_all(spectra, ORDER, 0, 0, tiled=True)  13.8 us
    all_to_all x1, starting transfers between devices, on_device(): moved = lax.all_to_all(spectra, ORDER, 0, 0, tiled=True)  11.2 us
    pallas_call x1, Pallas kernels, channelize(): pl.pallas_call(channel_kernel, grid=(antennas // PAIR,), in_specs=[pl.Blo...  9.35 us
    pallas_call x1, Pallas kernels, form_beams(): pl.pallas_call(beam_kernel, grid=(owned, beams // block), in_specs=[pl.Bl...  6.98 us
    pallas_call x1, Pallas kernels, dedisperse(): pl.pallas_call(dedisperse_kernel, in_specs=[pl.BlockSpec(memory_space=plt...  4.14 us
  transfers between devices with their start and end apart: 1, of which 1 were waited for; matrix products, arithmetic and copies ran while one was open for 0% of the time, Pallas kernels for 14%

profile of v4, /device:TPU:0, one launch (start us, length us, event | category | flops | bytes accessed | tf_op | source)
XLA Modules:
  0.0 98.3 jit_solution(7957330818679144325)
XLA Ops:
  0.6 0.0 copy-start.1
  0.6 9.3 %shard_map.77 = bf16[512,8,256]{2,1,0:T(8,128)(2,1)} custom-call(bf16[4,128,512]{2,1,0:T(8,128)(2,1)} %constant.4.clone.table_ref, bf16[256,256]{1,0:T(8,128)(2,1)} %constant.5.clone.mix_ref, bf16[32768,128]{1,0:T(8,128)(2,1)} %bitcast.11), custom_call_target="tpu_custom_call" | custom-call | tf_op jit(solution)/shard_map/pallas_call | solution.py:135
  10.0 11.2 %all-to-all-start = ((bf16[128,4,8,256]{3,2,1,0:T(8,128)(2,1)}), bf16[128,4,8,256]{3,2,1,0:T(8,128)(2,1)S(1)}, u32[]{:S(2)}, u32[]{:S(2)}) async-start(bf16[128,4,8,256]{3,2,1,0:T(8,128)(2,1)} %bitcast.12), calls=%async_computation | async-start | bytes 4194304 | tf_op jit(solution)/shard_map/all_to_all | solution.py:303
  21.2 0.0 copy-done.1
  21.2 0.1 reshape.25
  21.4 0.1 reshape_reshape.3.map_ref
  21.5 14.0 %shard_map.78.weight_ref = bf16[2,2,1024,1024]{3,2,1,0:T(8,128)(2,1)} custom-call(s32[1,1024]{1,0:T(1,128)S(1)} %reshape_reshape.3.map_ref, bf16[2,2,1024,1024]{3,2,1,0:T(8,128)(2,1)} %weight_ref.1), custom_call_target="tpu_custom_call" | custom-call | tf_op jit(solution)/shard_map/pallas_call | solution.py:191
  35.5 0.0 copy-start
  35.5 13.8 %all-to-all-done.spectra_ref = bf16[128,4,8,256]{3,2,1,0:T(8,128)(2,1)S(1)} async-done(((bf16[128,4,8,256]{3,2,1,0:T(8,128)(2,1)}), bf16[128,4,8,256]{3,2,1,0:T(8,128)(2,1)S(1)}, u32[]{:S(2)}, u32[]{:S(2)}) %all-to-all-start) | async-done | bytes 2097184 | tf_op jit(solution)/shard_map/all_to_all | solution.py:303
  49.3 7.0 %shard_map.79 = bf16[16,2,64,256]{3,2,1,0:T(8,128)(2,1)S(1)} custom-call(bf16[128,4,8,256]{3,2,1,0:T(8,128)(2,1)S(1)} %all-to-all-done.spectra_ref, bf16[2,2,1024,1024]{3,2,1,0:T(8,128)(2,1)} %shard_map.78.weight_ref), custom_call_target="tpu_custom_call" | custom-call | tf_op jit(solution)/shard_map/pallas_call | solution.py:206
  56.2 21.0 %all_to_all.15 = bf16[16,2,64,256]{3,2,1,0:T(8,128)(2,1)S(1)} all-to-all(bf16[16,2,64,256]{3,2,1,0:T(8,128)(2,1)S(1)} %shard_map.79), channel_id=1, replica_groups=mesh['zh'=2,'x'=4,'zl'=2,'y'=4,'core'=2] {'zl','y','core'}, dimensions={0} | all-to-all | bytes 2097152 | tf_op jit(solution)/shard_map/all_to_all | solution.py:307
  77.3 0.0 copy-done
  77.3 4.1 %shard_map.80 = (bf16[32,64,128]{2,1,0:T(8,128)(2,1)S(1)}, bf16[32,64,256]{2,1,0:T(8,128)(2,1)}) custom-call(s32[32,32]{1,0:T(8,128)S(1)} %copy-done, bf16[32,64,256]{2,1,0:T(8,128)(2,1)S(1)} %bitcast.9), custom_call_target="tpu_custom_call" | custom-call | tf_op jit(solution)/shard_map/pallas_call | solution.py:257
  81.4 14.9 %all_to_all.16.pieces_ref = bf16[8,4,64,128]{3,2,1,0:T(8,128)(2,1)} all-to-all(bf16[8,4,64,128]{3,2,1,0:T(8,128)(2,1)S(1)} %bitcast.10), channel_id=1, replica_groups=mesh['zh'=2,'x'=4,'zl'=2,'y'=4,'core'=2] {'zh','x'}, dimensions={0} | all-to-all | bytes 1048576 | tf_op jit(solution)/shard_map/all_to_all | solution.py:311
  96.4 1.9 %shard_map.81 = f32[4,64,128]{2,1,0:T(8,128)} custom-call(bf16[8,4,64,128]{3,2,1,0:T(8,128)(2,1)} %all_to_all.16.pieces_ref), custom_call_target="tpu_custom_call" | custom-call | tf_op jit(solution)/shard_map/pallas_call | solution.py:291
  (1 shorter events, 0.0 us)
Async XLA Ops:
  0.6 20.6 %copy-start.1 = (s32[1024]{0:T(1024)S(1)}, s32[1024]{0:T(1024)}, u32[]{:S(2)}) copy-start(s32[1024]{0:T(1024)} %param.8) | copy-start | bytes 12292
  10.0 39.3 %all-to-all-start = ((bf16[128,4,8,256]{3,2,1,0:T(8,128)(2,1)}), bf16[128,4,8,256]{3,2,1,0:T(8,128)(2,1)S(1)}, u32[]{:S(2)}, u32[]{:S(2)}) async-start(bf16[128,4,8,256]{3,2,1,0:T(8,128)(2,1)} %bitcast.12), calls=%async_computation | async-start | bytes 4194304 | tf_op jit(solution)/shard_map/all_to_all | solution.py:303
  35.5 41.8 %copy-start = (s32[32,32]{1,0:T(8,128)S(1)}, s32[32,32]{1,0:T(8,128)}, u32[]{:S(2)}) copy-start(s32[32,32]{1,0:T(8,128)} %delay_ref.1) | copy-start | bytes 12292

commit v5 on v4

--- a/solution.py
+++ b/solution.py
@@ -57,14 +57,14 @@
 
 
 def mix_frames(mix_ref, sample_ref, mixed_ref, row, p):
-    start = row + p * 512
-    block = jnp.concatenate([sample_ref[start : start + 256, :], sample_ref[start + 256 : start + 512, :]], axis=1)
+    start = row + p * 1024
+    block = jnp.concatenate([sample_ref[start + 256 * n : start + 256 * n + 256, :] for n in range(4)], axis=1)
     got = jnp.dot(mix_ref[...], block, preferred_element_type=jnp.float32).astype(jnp.bfloat16)
     for k in range(16):
         r, lane = k // 4, k % 4 * 128
-        for side in range(2):
-            first = p * 32 + side * 16
-            mixed_ref[r, first : first + 16, lane : lane + 128] = got[16 * k : 16 * k + 16, side * 128 : side * 128 + 128]
+        for n in range(4):
+            first = p * 64 + n * 16
+            mixed_ref[r, first : first + 16, lane : lane + 128] = got[16 * k : 16 * k + 16, n * 128 : n * 128 + 128]
 
 
 def transform(table_ref, mixed_ref, done_ref, antenna, r):
@@ -88,18 +88,12 @@
     last = PAIR * (pl.num_programs(0) - 1)
     before = jnp.where(antenna == 0, last + 1, antenna - 1)
 
-    @pl.when(antenna == 0)
-    def _():
-        mixed_b[...] = jnp.zeros(mixed_b.shape, mixed_b.dtype)
-
-    for p in range(8):
+    for p in range(4):
         mix_frames(mix_ref, sample_ref, mixed_a, 0, p)
-        if p % 2 == 0:
-            transform(table_ref, mixed_b, done_ref, before, p // 2)
-    for p in range(8):
+        transform(table_ref, mixed_b, done_ref, before, p)
+    for p in range(4):
         mix_frames(mix_ref, sample_ref, mixed_b, FR * 16, p)
-        if p % 2 == 0:
-            transform(table_ref, mixed_a, done_ref, antenna, p // 2)
+        transform(table_ref, mixed_a, done_ref, antenna, p)
 
     @pl.when(antenna == last)
     def _():
@@ -290,8 +284,10 @@
     beams = pieces.shape[3] // 2
     return pl.pallas_call(
         sum_kernel,
+        in_specs=[pl.BlockSpec(memory_space=pltpu.VMEM)],
+        out_specs=pl.BlockSpec(memory_space=pltpu.VMEM),
         out_shape=jax.ShapeDtypeStruct((pieces.shape[1], beams, OUT), jnp.float32),
-    )(pieces)
+    )(pltpu.with_memory_space_constraint(pieces, pltpu.VMEM))
 
 
 def on_device(voltages, weights, antenna_map, delays):

time: 98.9 us -> 97.6 us (0.987)
  Pallas kernels: 36.4 us -> 35.2 us
    pallas_call x1, Pallas kernels: 1.95 us -> 0.91 us  [sum_pieces(): pl.pallas_call(sum_kernel, in_specs=[pl.BlockSpec(memory_space=pltpu.VMEM...]
where the time goes in v5:
time: 97.6 us; the launch traced here: 97 us
  blocking collectives  35.9 us (37%)
  Pallas kernels  35.2 us (36%)
  waiting for transfers between devices  13.8 us (14%)
  starting transfers between devices  11.2 us (11%)
    all_to_all x1, blocking collectives, on_device(): filterbank = lax.all_to_all(power, beam, 0, 0, tiled=True)  21 us
    all_to_all x1, blocking collectives, on_device(): series = sum_pieces(lax.all_to_all(pieces, sub, 0, 0, tiled=True))  14.8 us
    pallas_call x1, Pallas kernels, order_weights(): pl.pallas_call(order_kernel, grid=(owned, beams // block), in_specs=[pl.B...  14 us
    all_to_all x1, waiting for transfers between devices, on_device(): moved = lax.all_to_all(spectra, ORDER, 0, 0, tiled=True)  13.8 us
    all_to_all x1, starting transfers between devices, on_device(): moved = lax.all_to_all(spectra, ORDER, 0, 0, tiled=True)  11.2 us
    pallas_call x1, Pallas kernels, channelize(): pl.pallas_call(channel_kernel, grid=(antennas // PAIR,), in_specs=[pl.Blo...  9.22 us
    pallas_call x1, Pallas kernels, form_beams(): pl.pallas_call(beam_kernel, grid=(owned, beams // block), in_specs=[pl.Bl...  6.97 us
    pallas_call x1, Pallas kernels, dedisperse(): pl.pallas_call(dedisperse_kernel, in_specs=[pl.BlockSpec(memory_space=plt...  4.13 us
  transfers between devices with their start and end apart: 1, of which 1 were waited for; matrix products, arithmetic and copies ran while one was open for 0% of the time, Pallas kernels for 14%

profile of v5, /device:TPU:0, one launch (start us, length us, event | category | flops | bytes accessed | tf_op | source)
XLA Modules:
  0.0 97.0 jit_solution(10669601007816528819)
XLA Ops:
  0.6 0.0 copy-start.1
  0.6 9.2 %shard_map.77 = bf16[512,8,256]{2,1,0:T(8,128)(2,1)} custom-call(bf16[4,128,512]{2,1,0:T(8,128)(2,1)} %constant.4.clone.table_ref, bf16[256,256]{1,0:T(8,128)(2,1)} %constant.5.clone.mix_ref, bf16[32768,128]{1,0:T(8,128)(2,1)} %bitcast.11), custom_call_target="tpu_custom_call" | custom-call | tf_op jit(solution)/shard_map/pallas_call | solution.py:129
  9.9 11.2 %all-to-all-start = ((bf16[128,4,8,256]{3,2,1,0:T(8,128)(2,1)}), bf16[128,4,8,256]{3,2,1,0:T(8,128)(2,1)S(1)}, u32[]{:S(2)}, u32[]{:S(2)}) async-start(bf16[128,4,8,256]{3,2,1,0:T(8,128)(2,1)} %bitcast.12), calls=%async_computation | async-start | bytes 4194304 | tf_op jit(solution)/shard_map/all_to_all | solution.py:299
  21.0 0.0 copy-done.1
  21.1 0.1 reshape.25
  21.3 0.1 reshape_reshape.3.map_ref
  21.4 14.0 %shard_map.78.weight_ref = bf16[2,2,1024,1024]{3,2,1,0:T(8,128)(2,1)} custom-call(s32[1,1024]{1,0:T(1,128)S(1)} %reshape_reshape.3.map_ref, bf16[2,2,1024,1024]{3,2,1,0:T(8,128)(2,1)} %weight_ref.1), custom_call_target="tpu_custom_call" | custom-call | tf_op jit(solution)/shard_map/pallas_call | solution.py:185
  35.4 0.0 copy-start
  35.4 13.8 %all-to-all-done.spectra_ref = bf16[128,4,8,256]{3,2,1,0:T(8,128)(2,1)S(1)} async-done(((bf16[128,4,8,256]{3,2,1,0:T(8,128)(2,1)}), bf16[128,4,8,256]{3,2,1,0:T(8,128)(2,1)S(1)}, u32[]{:S(2)}, u32[]{:S(2)}) %all-to-all-start) | async-done | bytes 2097184 | tf_op jit(solution)/shard_map/all_to_all | solution.py:299
  49.1 7.0 %shard_map.79 = bf16[16,2,64,256]{3,2,1,0:T(8,128)(2,1)S(1)} custom-call(bf16[128,4,8,256]{3,2,1,0:T(8,128)(2,1)S(1)} %all-to-all-done.spectra_ref, bf16[2,2,1024,1024]{3,2,1,0:T(8,128)(2,1)} %shard_map.78.weight_ref), custom_call_target="tpu_custom_call" | custom-call | tf_op jit(solution)/shard_map/pallas_call | solution.py:200
  56.1 21.0 %all_to_all.15 = bf16[16,2,64,256]{3,2,1,0:T(8,128)(2,1)S(1)} all-to-all(bf16[16,2,64,256]{3,2,1,0:T(8,128)(2,1)S(1)} %shard_map.79), channel_id=1, replica_groups=mesh['zh'=2,'x'=4,'zl'=2,'y'=4,'core'=2] {'zl','y','core'}, dimensions={0} | all-to-all | bytes 2097152 | tf_op jit(solution)/shard_map/all_to_all | solution.py:303
  77.1 0.0 copy-done
  77.1 4.1 %shard_map.80 = (bf16[32,64,128]{2,1,0:T(8,128)(2,1)S(1)}, bf16[32,64,256]{2,1,0:T(8,128)(2,1)}) custom-call(s32[32,32]{1,0:T(8,128)S(1)} %copy-done, bf16[32,64,256]{2,1,0:T(8,128)(2,1)S(1)} %bitcast.9), custom_call_target="tpu_custom_call" | custom-call | tf_op jit(solution)/shard_map/pallas_call | solution.py:251
  81.3 14.8 %all_to_all.16.pieces_ref = bf16[8,4,64,128]{3,2,1,0:T(8,128)(2,1)S(1)} all-to-all(bf16[8,4,64,128]{3,2,1,0:T(8,128)(2,1)S(1)} %bitcast.10), channel_id=1, replica_groups=mesh['zh'=2,'x'=4,'zl'=2,'y'=4,'core'=2] {'zh','x'}, dimensions={0} | all-to-all | bytes 1048576 | tf_op jit(solution)/shard_map/all_to_all | solution.py:307
  96.1 0.9 shard_map.81
  (1 shorter events, 0.0 us)
Async XLA Ops:
  0.6 20.4 %copy-start.1 = (s32[1024]{0:T(1024)S(1)}, s32[1024]{0:T(1024)}, u32[]{:S(2)}) copy-start(s32[1024]{0:T(1024)} %param.8) | copy-start | bytes 12292
  9.9 39.3 %all-to-all-start = ((bf16[128,4,8,256]{3,2,1,0:T(8,128)(2,1)}), bf16[128,4,8,256]{3,2,1,0:T(8,128)(2,1)S(1)}, u32[]{:S(2)}, u32[]{:S(2)}) async-start(bf16[128,4,8,256]{3,2,1,0:T(8,128)(2,1)} %bitcast.12), calls=%async_computation | async-start | bytes 4194304 | tf_op jit(solution)/shard_map/all_to_all | solution.py:299
  35.4 41.8 %copy-start = (s32[32,32]{1,0:T(8,128)S(1)}, s32[32,32]{1,0:T(8,128)}, u32[]{:S(2)}) copy-start(s32[32,32]{1,0:T(8,128)} %delay_ref.1) | copy-start | bytes 12292

commit v6 on v5

--- a/solution.py
+++ b/solution.py
@@ -211,28 +211,36 @@
     )(spectra, pltpu.with_memory_space_constraint(weights, pltpu.HBM))
 
 
-def dedisperse_kernel(delay_ref, power_ref, out_ref, kept_ref, turned_ref, sem):
-    channels, beams = power_ref.shape[:2]
-    keep = pltpu.make_async_copy(power_ref, kept_ref, sem)
-    keep.start()
+def dedisperse_kernel(delay_ref, core_ref, near_ref, far_ref, out_ref, kept_ref, turned_ref, sems):
+    chips, _, owned, beams = near_ref.shape[:4]
+    channels = chips * 2 * owned
+    core = core_ref[0]
+    copies = [
+        pltpu.make_async_copy(near_ref.at[:, core], kept_ref.at[:, core], sems.at[0]),
+        pltpu.make_async_copy(far_ref, kept_ref.at[:, 1 - core], sems.at[1]),
+    ]
+    for copy in copies:
+        copy.start()
     rows = lax.broadcasted_iota(jnp.int32, (ROWS, FR), 0)
     lanes = lax.broadcasted_iota(jnp.int32, (ROWS, FR), 1)
     unit = jnp.where(rows == lanes, 1.0, 0.0).astype(jnp.bfloat16)
 
-    for pair in range(channels // 2):
-        parts = []
-        for c in range(2):
-            power = power_ref[2 * pair + c]
-            parts += [power, jnp.concatenate([power[:, HALF:], power[:, :HALF]], axis=1)]
-        both = lax.dot_general(
-            unit,
-            jnp.concatenate(parts, axis=0),
-            (((1,), (1,)), ((), ())),
-            preferred_element_type=jnp.float32,
-        )
-        for c in range(2):
-            start = (2 * pair + c) * ROWS
-            turned_ref[start : start + ROWS, :] = both[:, c * 2 * beams : (c + 1) * 2 * beams]
+    for chip in range(chips):
+        for side in range(2):
+            parts = []
+            for k in range(owned):
+                power = near_ref[chip, core, k] if side == 0 else far_ref[chip, k]
+                parts += [power, jnp.concatenate([power[:, HALF:], power[:, :HALF]], axis=1)]
+            both = lax.dot_general(
+                unit,
+                jnp.concatenate(parts, axis=0),
+                (((1,), (1,)), ((), ())),
+                preferred_element_type=jnp.float32,
+            )
+            source = core if side == 0 else 1 - core
+            for k in range(owned):
+                start = pl.multiple_of(((chip * 2 + source) * owned + k) * ROWS, 8)
+                turned_ref[pl.ds(start, ROWS), :] = both[:, k * 2 * beams : (k + 1) * 2 * beams]
 
     def trial(pair, carry):
         for t in (2 * pair, 2 * pair + 1):
@@ -243,15 +251,19 @@
         return carry
 
     lax.fori_loop(0, TRIALS // 2, trial, 0)
-    keep.wait()
-
-
-def dedisperse(filterbank, delays):
-    channels, beams = filterbank.shape[:2]
+    for copy in copies:
+        copy.wait()
+
+
+def dedisperse(delays, core, near, far):
+    chips, _, owned, beams = near.shape[:4]
+    channels = chips * 2 * owned
     return pl.pallas_call(
         dedisperse_kernel,
         in_specs=[
             pl.BlockSpec(memory_space=pltpu.SMEM),
+            pl.BlockSpec(memory_space=pltpu.SMEM),
+            pl.BlockSpec(memory_space=pltpu.VMEM),
             pl.BlockSpec(memory_space=pltpu.VMEM),
         ],
         out_specs=(
@@ -260,14 +272,14 @@
         ),
         out_shape=(
             jax.ShapeDtypeStruct((TRIALS, HALF, 2 * beams), jnp.bfloat16),
-            jax.ShapeDtypeStruct(filterbank.shape, filterbank.dtype),
+            jax.ShapeDtypeStruct(near.shape, near.dtype),
         ),
         scratch_shapes=[
             pltpu.VMEM((channels * ROWS, 2 * beams), jnp.float32),
-            pltpu.SemaphoreType.DMA,
+            pltpu.SemaphoreType.DMA((2,)),
         ],
         compiler_params=pltpu.CompilerParams(vmem_limit_bytes=16 << 20),
-    )(delays, filterbank)
+    )(delays, core.reshape(1), near, far)
 
 
 def sum_kernel(pieces_ref, out_ref):
@@ -296,13 +308,19 @@
     owned = weights.shape[0]
     spectra = channelize(voltages)
     spectra = spectra.reshape(-1, owned * 2, voltages.shape[0], FR)
+    core = lax.axis_index("core")
+    spectra, core, delays = lax.optimization_barrier((spectra, core, delays))
     moved = lax.all_to_all(spectra, ORDER, 0, 0, tiled=True)
     arrived = antenna_map.reshape(*SIZES, -1).transpose(*TURN, len(SIZES)).reshape(A)
     ordered = order_weights(arrived, weights)
     power = form_beams(moved, ordered, beam_count)
-    filterbank = lax.all_to_all(power, beam, 0, 0, tiled=True)
+    power = power.reshape(beam_count // 2, 2, *power.shape[1:])
+    near = lax.all_to_all(power, ("zl", "y"), 0, 0, tiled=True)
+    near, core = lax.optimization_barrier((near, core))
+    away = lax.dynamic_index_in_dim(near, 1 - core, 1, keepdims=False)
+    far = lax.ppermute(away, "core", [(0, 1), (1, 0)])
+    partial, filterbank = dedisperse(delays, core, near, far)
     filterbank = filterbank.reshape(beam_count * owned, -1, FR)
-    partial, filterbank = dedisperse(filterbank, delays)
     pieces = partial.reshape(subband_count, TRIALS // subband_count, *partial.shape[1:])
     series = sum_pieces(lax.all_to_all(pieces, sub, 0, 0, tiled=True))
     return (filterbank, series)

time: 97.6 us -> 100 us (1.025)
  waiting for transfers between devices: 13.8 us -> 15.7 us
    ppermute x0 -> x1, waiting for transfers between devices: none -> 1.9 us  [on_device(): far = lax.ppermute(away, 'core', [(0, 1), (1, 0)])]
    all_to_all x1, blocking collectives: 14.8 us -> 16.6 us  [on_device(): series = sum_pieces(lax.all_to_all(pieces, sub, 0, 0, tiled=True))]
    all_to_all x1, blocking collectives: 21 us -> 19.7 us  [on_device(): near = lax.all_to_all(power, ('zl', 'y'), 0, 0, tiled=True)]
  transfers between devices with their start and end apart: 1 -> 2, of which waited for: 1 -> 2; matrix products, arithmetic and copies ran while one was open for 0% -> 0% of each run, Pallas kernels for 14% -> 14%
where the time goes in v6:
time: 100 us; the launch traced here: 99.6 us
  blocking collectives  36.3 us (36%)
  Pallas kernels  35.3 us (35%)
  waiting for transfers between devices  15.7 us (16%)
  starting transfers between devices  11.3 us (11%)
    all_to_all x1, blocking collectives, on_device(): near = lax.all_to_all(power, ('zl', 'y'), 0, 0, tiled=True)  19.7 us
    all_to_all x1, blocking collectives, on_device(): series = sum_pieces(lax.all_to_all(pieces, sub, 0, 0, tiled=True))  16.6 us
    pallas_call x1, Pallas kernels, order_weights(): pl.pallas_call(order_kernel, grid=(owned, beams // block), in_specs=[pl.B...  14 us
    all_to_all x1, waiting for transfers between devices, on_device(): moved = lax.all_to_all(spectra, ORDER, 0, 0, tiled=True)  13.8 us
    all_to_all x1, starting transfers between devices, on_device(): moved = lax.all_to_all(spectra, ORDER, 0, 0, tiled=True)  11.2 us
    pallas_call x1, Pallas kernels, channelize(): pl.pallas_call(channel_kernel, grid=(antennas // PAIR,), in_specs=[pl.Blo...  9.22 us
    pallas_call x1, Pallas kernels, form_beams(): pl.pallas_call(beam_kernel, grid=(owned, beams // block), in_specs=[pl.Bl...  6.98 us
    pallas_call x1, Pallas kernels, dedisperse(): pl.pallas_call(dedisperse_kernel, in_specs=[pl.BlockSpec(memory_space=plt...  4.19 us
  transfers between devices with their start and end apart: 2, of which 2 were waited for; matrix products, arithmetic and copies ran while one was open for 0% of the time, Pallas kernels for 14%

profile of v6, /device:TPU:0, one launch (start us, length us, event | category | flops | bytes accessed | tf_op | source)
XLA Modules:
  0.0 99.6 jit_solution(9132309083930041190)
XLA Ops:
  0.6 0.0 copy-start.1
  0.6 9.2 %shard_map.77 = bf16[512,8,256]{2,1,0:T(8,128)(2,1)} custom-call(bf16[4,128,512]{2,1,0:T(8,128)(2,1)} %constant.17.clone.table_ref, bf16[256,256]{1,0:T(8,128)(2,1)} %constant.18.clone.mix_ref, bf16[32768,128]{1,0:T(8,128)(2,1)} %bitcast.15), custom_call_target="tpu_custom_call" | custom-call | tf_op jit(solution)/shard_map/pallas_call | solution.py:129
  9.9 11.2 %all-to-all-start = ((bf16[128,4,8,256]{3,2,1,0:T(8,128)(2,1)}), bf16[128,4,8,256]{3,2,1,0:T(8,128)(2,1)S(1)}, u32[]{:S(2)}, u32[]{:S(2)}) async-start(bf16[128,4,8,256]{3,2,1,0:T(8,128)(2,1)} %bitcast.16), calls=%async_computation | async-start | bytes 4194304 | tf_op jit(solution)/shard_map/all_to_all | solution.py:313
  21.1 0.0 copy-done.1
  21.1 0.1 reshape.31
  21.3 0.1 reshape_reshape.3.map_ref
  21.4 14.0 %shard_map.78.weight_ref = bf16[2,2,1024,1024]{3,2,1,0:T(8,128)(2,1)} custom-call(s32[1,1024]{1,0:T(1,128)S(1)} %reshape_reshape.3.map_ref, bf16[2,2,1024,1024]{3,2,1,0:T(8,128)(2,1)} %weight_ref.1), custom_call_target="tpu_custom_call" | custom-call | tf_op jit(solution)/shard_map/pallas_call | solution.py:185
  35.4 0.0 copy-start
  35.4 13.8 %all-to-all-done.spectra_ref = bf16[128,4,8,256]{3,2,1,0:T(8,128)(2,1)S(1)} async-done(((bf16[128,4,8,256]{3,2,1,0:T(8,128)(2,1)}), bf16[128,4,8,256]{3,2,1,0:T(8,128)(2,1)S(1)}, u32[]{:S(2)}, u32[]{:S(2)}) %all-to-all-start) | async-done | bytes 2097184 | tf_op jit(solution)/shard_map/all_to_all | solution.py:313
  49.2 7.0 %shard_map.79 = bf16[16,2,64,256]{3,2,1,0:T(8,128)(2,1)S(1)} custom-call(bf16[128,4,8,256]{3,2,1,0:T(8,128)(2,1)S(1)} %all-to-all-done.spectra_ref, bf16[2,2,1024,1024]{3,2,1,0:T(8,128)(2,1)} %shard_map.78.weight_ref), custom_call_target="tpu_custom_call" | custom-call | tf_op jit(solution)/shard_map/pallas_call | solution.py:200
  56.1 19.7 %all_to_all.15.near_ref = bf16[8,2,2,64,256]{4,3,2,1,0:T(8,128)(2,1)S(1)} all-to-all(bf16[8,2,2,64,256]{4,3,2,1,0:T(8,128)(2,1)S(1)} %bitcast.13), channel_id=1, replica_groups=mesh['zh'=2,'x'=4,'zl'=2,'y'=4,'core'=2] {'zl','y'}, dimensions={0} | all-to-all | bytes 2097152 | tf_op jit(solution)/shard_map/all_to_all | solution.py:318
  75.9 0.1 collective-permute-start
  76.0 1.9 %collective-permute-done.far_ref = bf16[8,2,64,256]{3,2,1,0:T(8,128)(2,1)S(1)} collective-permute-done((bf16[8,2,64,256]{3,2,1,0:T(8,128)(2,1)S(1)}, bf16[8,2,64,256]{3,2,1,0:T(8,128)(2,1)S(1)}, u32[]{:S(2)}, u32[]{:S(2)}) %collective-permute-start) | collective-permute-done | bytes 524320 | tf_op jit(solution)/shard_map/ppermute | solution.py:321
  77.9 0.0 copy-done
  77.9 4.2 %shard_map.80 = (bf16[32,64,128]{2,1,0:T(8,128)(2,1)S(1)}, bf16[8,2,2,64,256]{4,3,2,1,0:T(8,128)(2,1)}) custom-call(s32[32,32]{1,0:T(8,128)S(1)} %copy-done, s32[1]{0:T(128)} %bitcast.6.core_ref, bf16[8,2,2,64,256]{4,3,2,1,0:T(8,128)(2,1)S(1)} %all_to_all.15.near_ref, bf16[8,2,64,256]{3,2,1,0:T(8,128)(2,1)S(1)} %collective-permute-done.far_ref), custom_call_target="tpu_custom_call" | custom-call | tf_op jit(solution)/shard_map/pallas_call | solution.py:261
  82.1 16.6 %all_to_all.16.pieces_ref = bf16[8,4,64,128]{3,2,1,0:T(8,128)(2,1)S(1)} all-to-all(bf16[8,4,64,128]{3,2,1,0:T(8,128)(2,1)S(1)} %bitcast.14), channel_id=1, replica_groups=mesh['zh'=2,'x'=4,'zl'=2,'y'=4,'core'=2] {'zh','x'}, dimensions={0} | all-to-all | bytes 1048576 | tf_op jit(solution)/shard_map/all_to_all | solution.py:325
  98.7 0.9 shard_map.81
  (2 shorter events, 0.1 us)
Async XLA Ops:
  0.6 20.4 %copy-start.1 = (s32[1024]{0:T(1024)S(1)}, s32[1024]{0:T(1024)}, u32[]{:S(2)}) copy-start(s32[1024]{0:T(1024)} %param.8) | copy-start | bytes 12292
  9.9 39.3 %all-to-all-start = ((bf16[128,4,8,256]{3,2,1,0:T(8,128)(2,1)}), bf16[128,4,8,256]{3,2,1,0:T(8,128)(2,1)S(1)}, u32[]{:S(2)}, u32[]{:S(2)}) async-start(bf16[128,4,8,256]{3,2,1,0:T(8,128)(2,1)} %bitcast.16), calls=%async_computation | async-start | bytes 4194304 | tf_op jit(solution)/shard_map/all_to_all | solution.py:313
  35.4 42.5 %copy-start = (s32[32,32]{1,0:T(8,128)S(1)}, s32[32,32]{1,0:T(8,128)}, u32[]{:S(2)}) copy-start(s32[32,32]{1,0:T(8,128)} %delay_ref) | copy-start | bytes 12292
  75.9 2.0 %collective-permute-start = (bf16[8,2,64,256]{3,2,1,0:T(8,128)(2,1)S(1)}, bf16[8,2,64,256]{3,2,1,0:T(8,128)(2,1)S(1)}, u32[]{:S(2)}, u32[]{:S(2)}) collective-permute-start(bf16[8,2,64,256]{3,2,1,0:T(8,128)(2,1)S(1)} %dynamic-slice_bitcast_fusion), channel_id=1, source_target_pairs={{0,1},{1,0},{2,3},{3,2},{4,5},{5,4},{6,7},{7,6},{8,9},{9,8},{10,11... | collective-permute-start | bytes 1572872 | tf_op jit(solution)/shard_map/ppermute | solution.py:321
